TPU v7x, 32 devices: a whole 2x2x4 slice. The times are simulated.
32 devices in a mesh: seq: 8 (over y, x, core), head: 4 (over z).
Axes of the slice: x: 2, y: 2, z: 4, core: 2. Of those that a mesh axis runs over, the one named last changes fastest.
Arguments:
- out_grad: bfloat16 [2048, 4096], P('seq', 'head'), may hold values from -7.2 to 7.2
- x_in: bfloat16 [2048, 4096], P('seq', 'head'), may hold values from -6 to 6
- b_in: bfloat16 [2048, 128], P('seq'), may hold values from -2.5 to 2.5
- c_in: bfloat16 [2048, 128], P('seq'), may hold values from -2.5 to 2.5
- dt_raw: float32 [64, 2048], P('head', 'seq'), may hold values from -5.1 to -0.7
- dt_bias: float32 [64], P('head'), may hold values from -0.5 to 0.5
- a_log: float32 [64], P('head'), may hold values from -7.5 to 2.2
- d_skip: float32 [64], P('head'), may hold values from 0.5 to 1.5
- states: bfloat16 [8, 4096, 128], P('seq', 'head'), may hold values from -6 to 6
- w_out: bfloat16 [4096, 4096], P('head'), may hold values from -0.09375 to 0.09375
- w_in: bfloat16 [4096, 4096], P(None, 'head'), may hold values from -0.125 to 0.125
Outputs:
- in_grad: bfloat16 [4096, 2048], P('head', 'seq')
- bc_grad: bfloat16 [256, 2048], P('head', 'seq')
- dt_grad: float32 [64, 2048], P('head', 'seq')
- param_grad: float32 [3, 64], P(None, 'head')
All inputs are finite; a program needn't handle non-finite values.
Results may differ from a plain program's by a relative error of at most 0.015.
Values may be sent and summed in bfloat16 or wider, within the bound.
A program may use at most 64 MiB of HBM per device.

v0:
```python
import jax
import jax.numpy as jnp
from jax import lax
from jax.sharding import PartitionSpec as P


def entering(value, axis, join, neutral):
    count, mine = (lax.axis_size(axis), lax.axis_index(axis))
    pieces = jax.tree.map(lambda part: lax.all_gather(part, axis), value)
    pieces = jax.tree.map(lambda part: part[::-1], pieces)
    mine = count - 1 - mine
    so_far = jax.tree.map(
        lambda part, zero: jnp.full_like(part, 0) + jnp.asarray(zero, part.dtype), value, neutral
    )

    def turn(position, so_far):
        longer = join(so_far, jax.tree.map(lambda part: part[position], pieces))
        return jax.tree.map(lambda new, old: jnp.where(position < mine, new, old), longer, so_far)

    return lax.fori_loop(0, count - 1, turn, so_far)


def shards(out_grad, x_in, b_in, c_in, dt_raw, dt_bias, a_log, d_skip, states, w_out, w_in):
    tokens_here, inner_here = x_in.shape
    group_heads = dt_raw.shape[0]
    head_dim = inner_here // group_heads
    state_dim = b_in.shape[1]
    contract_last = (((1,), (1,)), ((), ()))
    head_sum = lax.dot_general(
        lax.all_gather(out_grad, "head", axis=1, tiled=True),
        w_out,
        contract_last,
        preferred_element_type=jnp.float32,
    )
    dy_heads = head_sum.astype(jnp.bfloat16).reshape(tokens_here, group_heads, head_dim)
    dy_wide = dy_heads.astype(jnp.float32)
    x_heads = x_in.reshape(tokens_here, group_heads, head_dim)
    x_wide = x_heads.astype(jnp.float32)
    decay_rate = jnp.exp(a_log)
    step_size = jax.nn.softplus(dt_raw + dt_bias[:, None])
    log_step = -decay_rate[:, None] * step_size
    cumlog = jnp.cumsum(log_step, axis=1)
    positions = jnp.arange(tokens_here)
    causal = positions[:, None] >= positions[None, :]
    log_gaps = cumlog[:, :, None] - cumlog[:, None, :]
    decay_mask = jnp.where(causal[None], jnp.exp(jnp.minimum(log_gaps, 0.0)), 0.0)
    scores = lax.dot_general(c_in, b_in, contract_last, preferred_element_type=jnp.float32)
    step_rows = step_size.T
    x_scaled = (x_wide * step_rows[:, :, None]).astype(jnp.bfloat16)
    pair_dots = jnp.einsum("ihp,jhp->hij", dy_heads, x_scaled, preferred_element_type=jnp.float32)
    kernel = (scores[None] * decay_mask).astype(jnp.bfloat16)
    intra_back = jnp.einsum("hij,ihp->jhp", kernel, dy_heads, preferred_element_type=jnp.float32)
    masked_dots = (pair_dots * decay_mask).astype(jnp.bfloat16)
    start_decay = jnp.exp(cumlog)
    dy_decay = (dy_wide * start_decay.T[:, :, None]).astype(jnp.bfloat16)
    local_state = jnp.einsum("ihp,in->hpn", dy_decay, c_in, preferred_element_type=jnp.float32)
    end_total = jnp.exp(cumlog[:, -1])
    entry_state = states.reshape(group_heads, head_dim, state_dim)
    db_intra = jnp.einsum("hij,in->nj", masked_dots, c_in, preferred_element_type=jnp.float32)
    dc_intra = jnp.einsum("hij,jn->ni", masked_dots, b_in, preferred_element_type=jnp.float32)
    dc_entry = jnp.einsum("ihp,hpn->ni", dy_decay, entry_state, preferred_element_type=jnp.float32)
    ystate = jnp.einsum("in,hpn->ihp", c_in, entry_state, preferred_element_type=jnp.float32)
    pair_weight = pair_dots * scores[None] * decay_mask
    state_terms = start_decay * jnp.sum(dy_wide * ystate, axis=2).T
    skip_terms = jnp.sum(dy_wide * x_wide, axis=(0, 2))

    def compose(earlier, nearer):
        return (nearer[0] * earlier[0], nearer[0][:, None, None] * earlier[1] + nearer[1])

    identity_pair = (jnp.ones_like(end_total), jnp.zeros_like(local_state))
    carried = entering((end_total, local_state), "seq", compose, identity_pair)[1]
    carried_bf = carried.astype(jnp.bfloat16)
    state_back = jnp.einsum("jn,hpn->jhp", b_in, carried_bf, preferred_element_type=jnp.float32)
    end_decay = jnp.exp(cumlog[:, -1:] - cumlog)
    end_weight = (step_size * end_decay).T
    x_grad = (
        (
            step_rows[:, :, None] * intra_back
            + end_weight[:, :, None] * state_back
            + d_skip[None, :, None] * dy_wide
        )
        .astype(jnp.bfloat16)
        .reshape(tokens_here, inner_here)
    )
    x_end = (x_wide * end_weight[:, :, None]).astype(jnp.bfloat16)
    db_entry = jnp.einsum("jhp,hpn->nj", x_end, carried_bf, preferred_element_type=jnp.float32)
    bc_part = jnp.concatenate([db_intra + db_entry, dc_intra + dc_entry], axis=0)
    end_terms = end_weight.T * jnp.sum(x_wide * state_back, axis=2).T
    cum_grad = pair_weight.sum(axis=2) - pair_weight.sum(axis=1) + state_terms - end_terms
    tail_grad = end_terms.sum(axis=1) + end_total * jnp.sum(
        entry_state.astype(jnp.float32) * carried, axis=(1, 2)
    )
    cum_grad = cum_grad.at[:, -1].add(tail_grad)
    step_grad = jnp.cumsum(cum_grad[:, ::-1], axis=1)[:, ::-1]
    dt_sum = (
        -decay_rate[:, None] * step_grad
        + jnp.sum(x_wide * (intra_back + end_decay.T[:, :, None] * state_back), axis=2).T
    )
    dt_grad = dt_sum * jax.nn.sigmoid(dt_raw + dt_bias[:, None])
    param_terms = jnp.stack(
        [jnp.sum(step_grad * log_step, axis=1), skip_terms, jnp.sum(dt_grad, axis=1)]
    )
    in_part = lax.psum_scatter(
        lax.dot_general(w_in, x_grad, contract_last, preferred_element_type=jnp.float32).astype(
            jnp.bfloat16
        ),
        "head",
        scatter_dimension=0,
        tiled=True,
    )
    bc_sum = lax.psum_scatter(bc_part.astype(jnp.bfloat16), "head", scatter_dimension=0, tiled=True)
    norm_scale = (lax.axis_size("seq") * tokens_here * head_dim) ** (-0.5)
    param_grad = lax.psum(param_terms, "seq") * norm_scale
    return (in_part, bc_sum, dt_grad, param_grad)


def solution(mesh):
    return jax.shard_map(
        shards,
        mesh=mesh,
        in_specs=(
            P("seq", "head"),
            P("seq", "head"),
            P("seq", None),
            P("seq", None),
            P("head", "seq"),
            P("head"),
            P("head"),
            P("head"),
            P("seq", "head", None),
            P("head", None),
            P(None, "head"),
        ),
        out_specs=(P("head", "seq"), P("head", "seq"), P("head", "seq"), P(None, "head")),
        check_vma=False,
    )
```

profile of v0, /device:TPU:0, one launch (start us, length us, event | category | flops | bytes accessed | tf_op | source)
XLA Modules:
  0.0 200.9 jit_solution(2288571976925971934)
XLA Ops:
  9.2 0.8 copy_bitcast_fusion.3
  11.0 1.4 fusion.35
  12.9 45.1 %all-gather.5.cloned.1.call-done = bf16[256,4096]{1,0:T(8,128)(2,1)} async-done(((bf16[256,1024]{1,0:T(8,128)(2,1)}), bf16[256,4096]{1,0:T(8,128)(2,1)}) %all-gather.5.cloned.1.call-update) | async-done | bytes 2097168 | tf_op jit(solution)/shard_map/all_gather | solution.py:30
  58.0 7.8 %fusion.17 = (f32[1024]{0:T(1024)}, bf16[256,1024]{1,0:T(8,128)(2,1)}, bf16[256,1024]{1,0:T(8,128)(2,1)S(1)}) fusion(bf16[256,1024]{1,0:T(8,128)(2,1)} %param.16, f32[256,1024]{1,0:T(8,128)S(1)} %copy.72, bf16[256,4096]{1,0:T(8,128)(2,1)} %all-gather.5.cloned.1.call-done, bf16[1024,4096]{1,0:T(8,128)(2,1)} %param.24), kind=kOutput, calls=%fused_computation.36 | convolution fusion | flops 2149317632 | bytes 13111296 | tf_op jit(solution)/shard_map/dot_general | solution.py:29
  66.0 1.1 fusion.22
  68.9 13.9 %all-reduce = f32[128]{0:T(128)S(1)} all-reduce(f32[128]{0:T(128)S(1)} %dynamic-update-slice.3), channel_id=2, replica_groups=mesh['seq'=8,'head'=4] {'seq'}, use_global_device_ids=true, to_apply=%add | all-reduce | flops 128 | bytes 1024
  84.1 2.0 fusion.10
  86.1 16.6 %all-gather.7.cloned.1.call-done = f32[128,64,128]{2,1,0:T(8,128)} async-done(((f32[16,64,128]{2,1,0:T(8,128)}), f32[128,64,128]{2,1,0:T(8,128)}) %all-gather.7.cloned.1.call-update) | async-done | bytes 4194320 | tf_op jit(solution)/shard_map/all_gather | solution.py:9
  102.8 4.7 %rev.13 = f32[8,16,64,128]{3,2,1,0:T(8,128)} reverse(f32[8,16,64,128]{3,2,1,0:T(8,128)} %bitcast.136), dimensions={0} | reverse | bytes 8388608 | tf_op jit(solution)/shard_map/rev | solution.py:10
  107.5 13.2 %while.15 = (s32[]{:T(128)}, f32[16,64,128]{2,1,0:T(8,128)S(1)}, s32[]{:T(128)}, f32[8,16]{1,0:T(8,128)}, f32[8,16,64,128]{3,2,1,0:T(8,128)}, /*index=5*/s32[]{:T(128)}, s32[]{:T(128)}) while((s32[]{:T(128)}, f32[16,64,128]{2,1,0:T(8,128)S(1)}, s32[]{:T(128)}, f32[8,16]{1,0:T(8,128)}, f32[8,16,64,128]{3,2,1,0:T(8,128)}, ...), condition=%wide.region_3.4_spmd.clone, body=%wide.region_2.3_spmd.clone.sunk | while | flops 524292 | bytes 1573161 | solution.py:20
  107.5 0.7 dynamic-slice_bitcast_fusion.2
  108.2 1.2 fusion.62
  109.4 0.7 dynamic-slice_bitcast_fusion.2
  110.1 1.2 fusion.62
  111.3 0.7 dynamic-slice_bitcast_fusion.2
  112.0 1.2 fusion.62
  113.2 0.7 dynamic-slice_bitcast_fusion.2
  113.9 1.2 fusion.62
  115.0 0.7 dynamic-slice_bitcast_fusion.2
  115.7 1.2 fusion.62
  116.9 0.7 dynamic-slice_bitcast_fusion.2
  117.6 1.2 fusion.62
  119.5 1.2 fusion.62
  120.7 1.2 multiply_reduce_fusion.1
  121.9 7.2 %fusion.1 = bf16[4096,256]{0,1:T(8,128)(2,1)} fusion(bf16[256,1024]{0,1:T(8,128)(2,1)S(1)} %bitcast.142, bf16[4096,1024]{1,0:T(8,128)(2,1)} %param.25), kind=kOutput, calls=%fused_computation.4 | convolution fusion | flops 2148532224 | bytes 11010048 | tf_op jit(solution)/shard_map/dot_general | solution.py:104
  129.3 0.7 reduce_sum.127
  131.0 3.5 %fusion.2 = (f32[16,256]{1,0:T(8,128)S(1)}, f32[16,256]{1,0:T(8,128)S(1)}, bf16[256,256]{1,0:T(8,128)(2,1)S(1)}) fusion(f32[16,256]{1,0:T(8,128)} %copy-done.13, f32[256,256]{1,0:T(8,128)} %copy-done.5, pred[256,256]{1,0:T(8,128)(4,1)} %copy-done.15, bf16[256,16,64]{0,2,1:T(8,128)(2,1)S(1)} %bitcast.135, f32[256,16,64]{0,2,1:T(8,128)S(1)} %bitcast.130, ...), kind=kOutput, calls=%fused_computation.10 | convolution fusion | flops 146202624 | bytes 2097152 | tf_op jit(solution)/shard_map/ihp,jhp->hij/dot_general | solution.py:50
  137.8 0.8 fusion.42
  138.7 13.9 %psum.7 = f32[3,16]{1,0:T(4,128)S(1)} all-reduce(f32[3,16]{1,0:T(4,128)S(1)} %pad_maximum_fusion.1), channel_id=1, replica_groups=mesh['seq'=8,'head'=4] {'seq'}, use_global_device_ids=true, to_apply=%region_20.21 | all-reduce | flops 48 | bytes 384 | tf_op jit(solution)/shard_map/psum | solution.py:113
  153.2 19.8 %reduce-scatter.3.cloned.1.call-done = bf16[1024,256]{0,1:T(8,128)(2,1)} async-done(((bf16[4096,256]{0,1:T(8,128)(2,1)}), bf16[1024,256]{0,1:T(8,128)(2,1)}) %reduce-scatter.3.cloned.1.call-update) | async-done | bytes 524304 | tf_op jit(solution)/shard_map/reduce_scatter | solution.py:103
  173.0 2.0 %copy.78 = bf16[1024,256]{1,0:T(8,128)(2,1)} copy(bf16[1024,256]{0,1:T(8,128)(2,1)} %reduce-scatter.3.cloned.1.call-done) | data formatting | bytes 1048576
  175.0 19.4 %reduce-scatter.5.cloned.1.call-done = bf16[64,256]{1,0:T(8,128)(2,1)} async-done(((bf16[256,256]{1,0:T(8,128)(2,1)}), bf16[64,256]{1,0:T(8,128)(2,1)}) %reduce-scatter.5.cloned.1.call-update) | async-done | bytes 32784 | tf_op jit(solution)/shard_map/reduce_scatter | solution.py:111
  (106 shorter events, 11.6 us)
Async XLA Ops:
  7.2 76.3 %copy-start = (bf16[256,128]{1,0:T(8,128)(2,1)S(1)}, bf16[256,128]{1,0:T(8,128)(2,1)}, u32[]{:S(2)}) copy-start(bf16[256,128]{1,0:T(8,128)(2,1)} %param.17) | copy-start | bytes 196612
  7.2 50.8 %all-gather.5.cloned.1.call-start = ((), (), s32[]{:S(2)}) async-start(), calls=%async_computation.2 | async-start | bytes 2621440 | tf_op jit(solution)/shard_map/all_gather | solution.py:30
  7.9 94.9 %all-gather.7.cloned.1.call-start = ((), (), s32[]{:S(2)}) async-start(), calls=%async_computation.5 | async-start | bytes 4718592 | tf_op jit(solution)/shard_map/all_gather | solution.py:9
  8.6 0.5 copy-start.22
  10.8 55.0 %copy-start.16 = (f32[16,2]{0,1:T(2,128)}, f32[16,2]{0,1:T(2,128)S(1)}, u32[]{:S(2)}) copy-start(f32[16,2]{0,1:T(2,128)S(1)} %slice.34) | copy-start | bytes 388
  10.8 1.6 copy-start.13
  11.0 54.8 %copy-start.19 = (f32[16]{0:T(128)}, f32[16]{0:T(128)S(1)}, u32[]{:S(2)}) copy-start(f32[16]{0:T(128)S(1)} %get-tuple-element.154) | copy-start | bytes 196
  12.9 53.1 %copy-start.2 = (bf16[256,128]{1,0:T(8,128)(2,1)S(1)}, bf16[256,128]{1,0:T(8,128)(2,1)}, u32[]{:S(2)}) copy-start(bf16[256,128]{1,0:T(8,128)(2,1)} %param.18) | copy-start | bytes 196612
  12.9 54.3 %copy-start.3 = (bf16[256,1024]{1,0:T(8,128)(2,1)S(1)}, bf16[256,1024]{1,0:T(8,128)(2,1)}, u32[]{:S(2)}) copy-start(bf16[256,1024]{1,0:T(8,128)(2,1)} %param.16) | copy-start | bytes 1572868
  65.8 1.6 copy-start.26
  67.2 105.8 %reduce-scatter.3.cloned.1.call-start = ((), (), s32[]{:S(2)}) async-start(), calls=%async_computation.3 | async-start | bytes 2621440 | tf_op jit(solution)/shard_map/reduce_scatter | solution.py:103
  83.5 0.6 copy-start.15
  84.1 23.4 %copy-start.5 = (f32[256,256]{1,0:T(8,128)}, f32[256,256]{1,0:T(8,128)S(1)}, u32[]{:S(2)}) copy-start(f32[256,256]{1,0:T(8,128)S(1)} %fusion.44) | copy-start | bytes 786436
  107.5 13.2 %copy-start.7 = (f32[256,16]{0,1:T(8,128)S(1)}, f32[256,16]{0,1:T(8,128)}, u32[]{:S(2)}) copy-start(f32[256,16]{0,1:T(8,128)} %get-tuple-element.175) | copy-start | bytes 49156
  107.5 13.2 %copy-start.9 = (f32[256,16]{0,1:T(8,128)S(1)}, f32[256,16]{0,1:T(8,128)}, u32[]{:S(2)}) copy-start(f32[256,16]{0,1:T(8,128)} %get-tuple-element.176) | copy-start | bytes 49156
  107.5 13.2 %copy-start.10 = (f32[256,16]{0,1:T(8,128)S(1)}, f32[256,16]{0,1:T(8,128)}, u32[]{:S(2)}) copy-start(f32[256,16]{0,1:T(8,128)} %get-tuple-element.174) | copy-start | bytes 49156
  107.5 13.2 %copy-start.25 = (f32[16]{0:T(128)S(1)}, f32[16]{0:T(128)}, u32[]{:S(2)}) copy-start(f32[16]{0:T(128)} %param.22) | copy-start | bytes 196
  121.9 7.3 %copy-start.21 = (f32[1024]{0:T(1024)S(1)}, f32[1024]{0:T(1024)}, u32[]{:S(2)}) copy-start(f32[1024]{0:T(1024)} %get-tuple-element.169) | copy-start | bytes 12292
  121.9 8.1 %copy-start.4 = (bf16[256,1024]{1,0:T(8,128)(2,1)S(1)}, bf16[256,1024]{1,0:T(8,128)(2,1)}, u32[]{:S(2)}) copy-start(bf16[256,1024]{1,0:T(8,128)(2,1)} %get-tuple-element.170) | copy-start | bytes 1572868
  121.9 8.3 %copy-start.1 = (bf16[1,1024,128]{2,1,0:T(8,128)(2,1)S(1)}, bf16[1,1024,128]{2,1,0:T(8,128)(2,1)}, u32[]{:S(2)}) copy-start(bf16[1,1024,128]{2,1,0:T(8,128)(2,1)} %param.23) | copy-start | bytes 786436
  129.2 65.2 %reduce-scatter.5.cloned.1.call-start = ((), (), s32[]{:S(2)}) async-start(), calls=%async_computation.4 | async-start | bytes 163840 | tf_op jit(solution)/shard_map/reduce_scatter | solution.py:111
  130.8 3.8 %copy-start.6 = (f32[16,256]{1,0:T(8,128)S(1)}, f32[16,256]{1,0:T(8,128)}, u32[]{:S(2)}) copy-start(f32[16,256]{1,0:T(8,128)} %param.19) | copy-start | bytes 49156
  130.9 3.8 %copy-start.11 = (f32[256,16]{0,1:T(8,128)S(1)}, f32[256,16]{0,1:T(8,128)}, u32[]{:S(2)}) copy-start(f32[256,16]{0,1:T(8,128)} %get-tuple-element.152) | copy-start | bytes 49156
  130.9 3.8 %copy-start.17 = (f32[16,2]{0,1:T(2,128)S(1)}, f32[16,2]{0,1:T(2,128)}, u32[]{:S(2)}) copy-start(f32[16,2]{0,1:T(2,128)} %copy-done.16) | copy-start | bytes 388
  130.9 3.8 %copy-start.18 = (f32[16]{0:T(128)S(1)}, f32[16]{0:T(128)}, u32[]{:S(2)}) copy-start(f32[16]{0:T(128)} %param.20) | copy-start | bytes 196
  130.9 3.8 %copy-start.20 = (f32[16]{0:T(128)S(1)}, f32[16]{0:T(128)}, u32[]{:S(2)}) copy-start(f32[16]{0:T(128)} %copy-done.19) | copy-start | bytes 196
  130.9 4.4 %copy-start.14 = (f32[16,256]{1,0:T(8,128)S(1)}, f32[16,256]{1,0:T(8,128)}, u32[]{:S(2)}) copy-start(f32[16,256]{1,0:T(8,128)} %copy-done.13) | copy-start | bytes 49156
  130.9 5.8 %copy-start.8 = (f32[256,16]{0,1:T(8,128)S(1)}, f32[256,16]{0,1:T(8,128)}, u32[]{:S(2)}) copy-start(f32[256,16]{0,1:T(8,128)} %get-tuple-element.175) | copy-start | bytes 49156
  130.9 6.9 %copy-start.12 = (f32[256,16]{0,1:T(8,128)S(1)}, f32[256,16]{0,1:T(8,128)}, u32[]{:S(2)}) copy-start(f32[256,16]{0,1:T(8,128)} %get-tuple-element.153) | copy-start | bytes 49156
  130.9 6.9 %copy-start.23 = (f32[16]{0:T(128)S(1)}, f32[16]{0:T(128)}, u32[]{:S(2)}) copy-start(f32[16]{0:T(128)} %copy-done.22) | copy-start | bytes 196
  130.9 7.7 %copy-start.24 = (f32[16]{0:T(128)S(1)}, f32[16]{0:T(128)}, u32[]{:S(2)}) copy-start(f32[16]{0:T(128)} %reduce_sum.127) | copy-start | bytes 196
Sparse Core Ops, SparseCore 0:
  9.6 48.3 all-gather.4
  67.3 35.4 all-gather.6
  129.3 43.6 reduce-scatter.2
  175.7 18.6 reduce-scatter.4
where the time goes:
time: 202 us; the launch traced here: 201 us
  waiting for transfers between devices  102 us (50%)
  blocking collectives  27.8 us (14%)
  matrix products  24.4 us (12%)
  local copies, waits for them, and re-layouts  16.4 us (8%)
  other arithmetic  15.7 us (8%)
  between operations  14.7 us (7%)
    all_gather x1, waiting for transfers between devices, shards(): lax.all_gather(out_grad, 'head', axis=1, tiled=True)  45.1 us
    reduce_scatter x1, waiting for transfers between devices, shards(): lax.psum_scatter(lax.dot_general(w_in, x_grad, contract_last, preferred_e...  19.8 us
    reduce_scatter x1, waiting for transfers between devices, shards(): lax.psum_scatter(bc_part.astype(jnp.bfloat16), 'head', scatter_dimension=...  19.4 us
    all_gather x1, waiting for transfers between devices, entering(): pieces = jax.tree.map(lambda part: lax.all_gather(part, axis), value)  16.6 us
    unnamed x1, blocking collectives  13.9 us
    psum x1, blocking collectives, shards(): param_grad = lax.psum(param_terms, 'seq') * norm_scale  13.9 us
    select_n x7, other arithmetic, turn(): jnp.where(position < mine, new, old)  8.18 us
    dot_general x1, matrix products, shards(): lax.dot_general(lax.all_gather(out_grad, 'head', axis=1, tiled=True), w_o...  7.83 us
  transfers between devices with their start and end apart: 4, of which 4 were waited for; matrix products, arithmetic and copies ran while one was open for 10% of the time, Pallas kernels for 0%

commit v1 on v0

--- a/solution.py
+++ b/solution.py
@@ -4,20 +4,39 @@
 from jax.sharding import PartitionSpec as P
 
 
-def entering(value, axis, join, neutral):
+def partners(count, distance):
+    return [(place, place ^ distance) for place in range(count)]
+
+
+def entering(decay, state, axis):
     count, mine = (lax.axis_size(axis), lax.axis_index(axis))
-    pieces = jax.tree.map(lambda part: lax.all_gather(part, axis), value)
-    pieces = jax.tree.map(lambda part: part[::-1], pieces)
-    mine = count - 1 - mine
-    so_far = jax.tree.map(
-        lambda part, zero: jnp.full_like(part, 0) + jnp.asarray(zero, part.dtype), value, neutral
-    )
+    carried = jnp.zeros_like(state)
+    reach = jnp.ones_like(decay)
+    distance = 1
+    while distance < count:
+        pairs = partners(count, distance)
+        other_decay = lax.ppermute(decay, axis, pairs)
+        other_state = lax.ppermute(state.astype(jnp.bfloat16), axis, pairs).astype(jnp.float32)
+        earlier = (mine // distance) % 2 == 0
+        carried = jnp.where(earlier, carried + reach[:, None, None] * other_state, carried)
+        reach = jnp.where(earlier, reach * other_decay, reach)
+        state = jnp.where(
+            earlier,
+            state + decay[:, None, None] * other_state,
+            other_state + other_decay[:, None, None] * state,
+        )
+        decay = decay * other_decay
+        distance *= 2
+    return carried
 
-    def turn(position, so_far):
-        longer = join(so_far, jax.tree.map(lambda part: part[position], pieces))
-        return jax.tree.map(lambda new, old: jnp.where(position < mine, new, old), longer, so_far)
 
-    return lax.fori_loop(0, count - 1, turn, so_far)
+def summed(value, axis):
+    count = lax.axis_size(axis)
+    distance = 1
+    while distance < count:
+        value = value + lax.ppermute(value, axis, partners(count, distance))
+        distance *= 2
+    return value
 
 
 def shards(out_grad, x_in, b_in, c_in, dt_raw, dt_bias, a_log, d_skip, states, w_out, w_in):
@@ -64,11 +83,7 @@
     state_terms = start_decay * jnp.sum(dy_wide * ystate, axis=2).T
     skip_terms = jnp.sum(dy_wide * x_wide, axis=(0, 2))
 
-    def compose(earlier, nearer):
-        return (nearer[0] * earlier[0], nearer[0][:, None, None] * earlier[1] + nearer[1])
-
-    identity_pair = (jnp.ones_like(end_total), jnp.zeros_like(local_state))
-    carried = entering((end_total, local_state), "seq", compose, identity_pair)[1]
+    carried = entering(end_total, local_state, "seq")
     carried_bf = carried.astype(jnp.bfloat16)
     state_back = jnp.einsum("jn,hpn->jhp", b_in, carried_bf, preferred_element_type=jnp.float32)
     end_decay = jnp.exp(cumlog[:, -1:] - cumlog)
@@ -100,17 +115,24 @@
     param_terms = jnp.stack(
         [jnp.sum(step_grad * log_step, axis=1), skip_terms, jnp.sum(dt_grad, axis=1)]
     )
-    in_part = lax.psum_scatter(
-        lax.dot_general(w_in, x_grad, contract_last, preferred_element_type=jnp.float32).astype(
-            jnp.bfloat16
-        ),
-        "head",
-        scatter_dimension=0,
-        tiled=True,
+    heads_count = lax.axis_size("head")
+    in_term = lax.dot_general(
+        w_in, x_grad, contract_last, preferred_element_type=jnp.float32
+    ).astype(jnp.bfloat16)
+    rows_here = in_term.shape[0] // heads_count
+    both = jnp.concatenate(
+        [
+            in_term.reshape(heads_count, rows_here, tokens_here),
+            bc_part.astype(jnp.bfloat16).reshape(heads_count, -1, tokens_here),
+        ],
+        axis=1,
     )
-    bc_sum = lax.psum_scatter(bc_part.astype(jnp.bfloat16), "head", scatter_dimension=0, tiled=True)
+    both_sum = lax.psum_scatter(
+        both.reshape(-1, tokens_here), "head", scatter_dimension=0, tiled=True
+    )
+    in_part, bc_sum = (both_sum[:rows_here], both_sum[rows_here:])
     norm_scale = (lax.axis_size("seq") * tokens_here * head_dim) ** (-0.5)
-    param_grad = lax.psum(param_terms, "seq") * norm_scale
+    param_grad = summed(param_terms, "seq") * norm_scale
     return (in_part, bc_sum, dt_grad, param_grad)
 
 

time: 202 us -> 162 us (0.80)
  blocking collectives: 27.8 us -> 0 us
  waiting for transfers between devices: 102 us -> 78.4 us
  starting transfers between devices: 0.16 us -> 9.59 us
  local copies, waits for them, and re-layouts: 16.4 us -> 21.4 us
  other arithmetic: 15.7 us -> 10.9 us
  matrix products: 24.4 us -> 26.6 us
    all_gather x1 -> x0, waiting for transfers between devices: 16.6 us -> none  [entering(): pieces = jax.tree.map(lambda part: lax.all_gather(part, axis), value)]
    ppermute x0 -> x8, waiting for transfers between devices: none -> 15 us  [the longest x3 9.91 us: entering(): lax.ppermute(state.astype(jnp.bfloat16), axis, pairs).astype(jnp.float32)]
    unnamed x1 -> x0, blocking collectives: 13.9 us -> none
    psum x1 -> x0, blocking collectives: 13.9 us -> none  [shards(): param_grad = lax.psum(param_terms, 'seq') * norm_scale]
    reduce_scatter x2 -> x1, waiting for transfers between devices: 39.2 us -> 28.2 us  [shards(): lax.psum_scatter(both.reshape(-1, tokens_here), 'head', scatter_dimension...]
    all_gather x1, waiting for transfers between devices: 45.1 us -> 34.5 us  [shards(): lax.all_gather(out_grad, 'head', axis=1, tiled=True)]
    ppermute x0 -> x8, starting transfers between devices: none -> 9.52 us  [the longest x2 3.51 us: entering(): other_decay = lax.ppermute(decay, axis, pairs)]
    select_n x7 -> x1, other arithmetic: 8.18 us -> 0.6 us  [entering(): reach = jnp.where(earlier, reach * other_decay, reach)]
  transfers between devices with their start and end apart: 4 -> 10, of which waited for: 4 -> 8; matrix products, arithmetic and copies ran while one was open for 10% -> 17% of each run, Pallas kernels for 0% -> 0%
where the time goes in v1:
time: 162 us; the launch traced here: 161 us
  waiting for transfers between devices  78.4 us (48%)
  matrix products  26.6 us (16%)
  local copies, waits for them, and re-layouts  21.4 us (13%)
  between operations  14.4 us (9%)
  other arithmetic  10.9 us (7%)
  starting transfers between devices  9.59 us (6%)
    all_gather x1, waiting for transfers between devices, shards(): lax.all_gather(out_grad, 'head', axis=1, tiled=True)  34.5 us
    reduce_scatter x1, waiting for transfers between devices, shards(): lax.psum_scatter(both.reshape(-1, tokens_here), 'head', scatter_dimension...  28.2 us
    ppermute x3, waiting for transfers between devices, entering(): lax.ppermute(state.astype(jnp.bfloat16), axis, pairs).astype(jnp.float32)  9.91 us
    dot_general x1, matrix products, shards(): lax.dot_general(lax.all_gather(out_grad, 'head', axis=1, tiled=True), w_o...  7.21 us
    dot_general x1, matrix products, shards(): lax.dot_general(w_in, x_grad, contract_last, preferred_element_type=jnp.f...  5.8 us
    ppermute x3, waiting for transfers between devices, summed(): value = value + lax.ppermute(value, axis, partners(count, distance))  4.97 us
    dot_general x1, matrix products, shards(): jnp.einsum('ihp,jhp->hij', dy_heads, x_scaled, preferred_element_type=jnp...  4 us
    concatenate x1, local copies, waits for them, and re-layouts, shards(): jnp.concatenate([in_term.reshape(heads_count, rows_here, tokens_here), bc...  3.55 us
  transfers between devices with their start and end apart: 10, of which 8 were waited for; matrix products, arithmetic and copies ran while one was open for 17% of the time, Pallas kernels for 0%

profile of v1, /device:TPU:0, one launch (start us, length us, event | category | flops | bytes accessed | tf_op | source)
XLA Modules:
  0.0 161.3 jit_solution(2156898000324561240)
XLA Ops:
  8.0 0.8 copy.92
  11.8 0.8 fusion.36
  15.3 1.0 fusion.53
  16.4 1.3 copy.102
  17.8 3.0 %collective-permute-start.3 = (f32[16]{0:T(128)S(1)}, f32[16]{0:T(128)S(1)}, u32[]{:S(2)}, u32[]{:S(2)}) collective-permute-start(f32[16]{0:T(128)S(1)} %fusion.46), channel_id=1, source_target_pairs={{0,8},{4,12},{8,0},{12,4},{16,24},{20,28},{24,16},{28,20},{1,9},{5... | collective-permute-start | bytes 200 | tf_op jit(solution)/shard_map/ppermute | solution.py:18
  20.8 1.3 copy.103
  23.5 34.5 %all-gather.2.cloned.1.call-done = bf16[256,4096]{1,0:T(8,128)(2,1)} async-done(((bf16[256,1024]{1,0:T(8,128)(2,1)}), bf16[256,4096]{1,0:T(8,128)(2,1)}) %all-gather.2.cloned.1.call-update) | async-done | bytes 2097168 | tf_op jit(solution)/shard_map/all_gather | solution.py:49
  58.0 7.2 %fusion.16 = (f32[1024]{0:T(1024)}, bf16[256,1024]{1,0:T(8,128)(2,1)S(1)}, bf16[256,1024]{1,0:T(8,128)(2,1)S(1)}) fusion(bf16[256,1024]{1,0:T(8,128)(2,1)S(1)} %copy-done.4, f32[256,1024]{1,0:T(8,128)} %copy.103, bf16[256,4096]{1,0:T(8,128)(2,1)} %all-gather.2.cloned.1.call-done, bf16[1024,4096]{1,0:T(8,128)(2,1)} %param.22), kind=kOutput, calls=%fused_computation.34 | convolution fusion | flops 2149317632 | bytes 13111296 | tf_op jit(solution)/shard_map/dot_general | solution.py:48
  66.1 4.0 %fusion.1 = (f32[16,256]{1,0:T(8,128)}, f32[16,256]{1,0:T(8,128)}, bf16[256,256]{1,0:T(8,128)(2,1)S(1)}) fusion(f32[16,256]{1,0:T(8,128)} %copy-done.7, f32[256,256]{1,0:T(8,128)S(1)} %fusion.53, pred[256,256]{1,0:T(8,128)(4,1)} %iota_compare_fusion, bf16[256,16,64]{0,2,1:T(8,128)(2,1)S(1)} %bitcast.112, f32[256,16,64]{0,2,1:T(8,128)S(1)} %bitcast.118, ...), kind=kOutput, calls=%fused_computation.7 | convolution fusion | flops 146202624 | bytes 2097152 | tf_op jit(solution)/shard_map/ihp,jhp->hij/dot_general | solution.py:69
  70.3 1.5 collective-permute-start.2
  71.9 3.2 %fusion.9 = f32[256,16,64]{0,2,1:T(8,128)} fusion(bf16[256,16,64]{0,2,1:T(8,128)(2,1)S(1)} %bitcast.113, f32[16,256]{1,0:T(8,128)S(1)} %copy-done.8, f32[256,256]{1,0:T(8,128)} %copy-done.6, pred[256,256]{1,0:T(8,128)(4,1)S(1)} %copy-done.9), kind=kOutput, calls=%fused_computation.19 | convolution fusion | flops 139460608 | bytes 1916928 | tf_op jit(solution)/shard_map/hij,ihp->jhp/dot_general | solution.py:71
  75.1 4.0 %collective-permute-done.2 = bf16[16,64,128]{2,1,0:T(8,128)(2,1)S(1)} collective-permute-done((bf16[16,64,128]{2,1,0:T(8,128)(2,1)S(1)}, bf16[16,64,128]{2,1,0:T(8,128)(2,1)S(1)}, u32[]{:S(2)}, u32[]{:S(2)}) %collective-permute-start.2) | collective-permute-done | bytes 262176 | tf_op jit(solution)/shard_map/ppermute | solution.py:19
  79.4 1.5 collective-permute-start.4
  81.5 5.9 %collective-permute-done.4 = bf16[16,64,128]{2,1,0:T(8,128)(2,1)S(1)} collective-permute-done((bf16[16,64,128]{2,1,0:T(8,128)(2,1)S(1)}, bf16[16,64,128]{2,1,0:T(8,128)(2,1)S(1)}, u32[]{:S(2)}, u32[]{:S(2)}) %collective-permute-start.4) | collective-permute-done | bytes 262176 | tf_op jit(solution)/shard_map/ppermute | solution.py:19
  88.1 0.9 copy.105
  88.9 2.6 %multiply_reduce_fusion.1 = (f32[256,16]{0,1:T(8,128)}, f32[256,16]{0,1:T(8,128)}, bf16[256,16,64]{0,2,1:T(8,128)(2,1)S(1)}) fusion(f32[256,1024]{0,1:T(8,128)S(1)} %copy.102, f32[256,16,64]{0,2,1:T(8,128)} %fusion.9, f32[256,16]{0,1:T(8,128)S(1)} %copy-done.10, bf16[256,1024]{0,1:T(8,128)(2,1)S(1)} %copy.94, f32[16]{0:T(128)} %param.20, ...), kind=kOutput, calls=%fused_computation.39 | convolution fusion | flops 71950336 | bytes 4079811 | tf_op jit(solution)/shard_map/jn,hpn->jhp/dot_general | solution.py:88
  91.6 5.8 %fusion = bf16[4096,256]{0,1:T(8,128)(2,1)S(1)} fusion(bf16[256,1024]{0,1:T(8,128)(2,1)S(1)} %bitcast.133, bf16[4096,1024]{1,0:T(8,128)(2,1)} %param.23), kind=kOutput, calls=%fused_computation.1 | convolution fusion | flops 2148532224 | bytes 11010048 | tf_op jit(solution)/shard_map/dot_general | solution.py:119
  97.4 2.8 %reshape.138 = bf16[4,1024,256]{1,0,2:T(4,128)(2,1)} reshape(bf16[4096,256]{0,1:T(8,128)(2,1)S(1)} %fusion) | data formatting | bytes 4194304 | tf_op jit(solution)/shard_map/reshape | solution.py:125
  100.2 2.8 %pad_maximum_fusion = bf16[4,1088,256]{1,0,2:T(4,128)(2,1)S(1)} fusion(bf16[4,64,256]{1,0,2:T(4,128)(2,1)} %copy.105, bf16[4,1024,256]{1,0,2:T(4,128)(2,1)} %reshape.138), kind=kLoop, calls=%fused_computation.9 | loop fusion | flops 4456448 | bytes 4456448 | tf_op jit(solution)/shard_map/concatenate | solution.py:123
  103.0 3.6 %copy.106 = bf16[4,1088,256]{2,1,0:T(8,128)(2,1)} copy(bf16[4,1088,256]{1,0,2:T(4,128)(2,1)S(1)} %pad_maximum_fusion) | data formatting | bytes 4456448 | tf_op jit(solution)/shard_map/concatenate | solution.py:123
  107.5 1.3 fusion.10
  108.8 0.8 copy.108
  109.7 0.8 copy.110
  110.6 1.6 %multiply_reduce_fusion.2 = f32[16]{0:T(128)S(1)} fusion(bf16[16,64,128]{2,1,0:T(8,128)(2,1)} %bitcast.116, bf16[16,64,128]{2,1,0:T(8,128)(2,1)} %copy-done.5, f32[16]{0:T(128)} %get-tuple-element.35, bf16[16,64,128]{2,1,0:T(8,128)(2,1)} %copy-done.2, f32[16]{0:T(128)} %get-tuple-element.36, bf16[16,64,128]{2,1,0:T(8,128)(2,1)S(1)} %collective-permute-done, ...), kind=kLoop, calls=%fused_computation.57 | loop fusion | flops 1703920 | bytes 1048771 | tf_op jit(solution)/shard_map/reduce_sum | solution.py:105
  114.0 1.1 collective-permute-done.5
  115.1 1.4 collective-permute-start.6
  116.5 2.2 %collective-permute-done.6 = f32[3,16]{1,0:T(4,128)S(1)} collective-permute-done((f32[3,16]{1,0:T(4,128)S(1)}, f32[3,16]{1,0:T(4,128)S(1)}, u32[]{:S(2)}, u32[]{:S(2)}) %collective-permute-start.6) | collective-permute-done | bytes 224 | tf_op jit(solution)/shard_map/ppermute | solution.py:37
  118.8 1.4 collective-permute-start.7
  120.9 1.6 collective-permute-done.7
  123.0 28.2 %reduce-scatter.2.cloned.1.call-done = bf16[1088,256]{1,0:T(8,128)(2,1)} async-done(((bf16[4352,256]{1,0:T(8,128)(2,1)}), bf16[1088,256]{1,0:T(8,128)(2,1)}) %reduce-scatter.2.cloned.1.call-update) | async-done | bytes 557072 | tf_op jit(solution)/shard_map/reduce_scatter | solution.py:130
  151.2 1.4 slice.50
  152.6 1.9 %slice.49 = bf16[1024,256]{1,0:T(8,128)(2,1)} slice(bf16[1088,256]{1,0:T(8,128)(2,1)} %reduce-scatter.2.cloned.1.call-done), slice={[0:1024], [0:256]} | slice | bytes 1048576 | tf_op jit(solution)/shard_map/slice | solution.py:133
  (120 shorter events, 14.5 us)
Async XLA Ops:
  7.2 8.2 %copy-start = (bf16[256,128]{1,0:T(8,128)(2,1)S(1)}, bf16[256,128]{1,0:T(8,128)(2,1)}, u32[]{:S(2)}) copy-start(bf16[256,128]{1,0:T(8,128)(2,1)} %param.15) | copy-start | bytes 196612
  7.2 50.8 %copy-start.4 = (bf16[256,1024]{1,0:T(8,128)(2,1)S(1)}, bf16[256,1024]{1,0:T(8,128)(2,1)}, u32[]{:S(2)}) copy-start(bf16[256,1024]{1,0:T(8,128)(2,1)} %param.14) | copy-start | bytes 1572868
  7.2 50.8 %all-gather.2.cloned.1.call-start = ((), (), s32[]{:S(2)}) async-start(), calls=%async_computation.1 | async-start | bytes 2621440 | tf_op jit(solution)/shard_map/all_gather | solution.py:49
  7.9 143.3 %reduce-scatter.2.cloned.1.call-start = ((), (), s32[]{:S(2)}) async-start(), calls=%async_computation.2 | async-start | bytes 2785280 | tf_op jit(solution)/shard_map/reduce_scatter | solution.py:130
  11.3 11.0 %copy-start.19 = (f32[16]{0:T(128)}, f32[16]{0:T(128)S(1)}, u32[]{:S(2)}) copy-start(f32[16]{0:T(128)S(1)} %fusion.45) | copy-start | bytes 196
  11.3 6.5 %collective-permute-start.1 = (f32[16]{0:T(128)S(1)}, f32[16]{0:T(128)S(1)}, u32[]{:S(2)}, u32[]{:S(2)}) collective-permute-start(f32[16]{0:T(128)S(1)} %fusion.45), channel_id=1, source_target_pairs={{0,4},{4,0},{8,12},{12,8},{16,20},{20,16},{24,28},{28,24},{1,5},{5... | collective-permute-start | bytes 200 | tf_op jit(solution)/shard_map/ppermute | solution.py:18
  16.4 49.7 %copy-start.6 = (f32[256,256]{1,0:T(8,128)}, f32[256,256]{1,0:T(8,128)S(1)}, u32[]{:S(2)}) copy-start(f32[256,256]{1,0:T(8,128)S(1)} %fusion.53) | copy-start | bytes 786436
  17.7 4.5 %copy-start.15 = (f32[16]{0:T(128)}, f32[16]{0:T(128)S(1)}, u32[]{:S(2)}) copy-start(f32[16]{0:T(128)S(1)} %collective-permute-done.1) | copy-start | bytes 196
  17.8 4.5 %collective-permute-start.3 = (f32[16]{0:T(128)S(1)}, f32[16]{0:T(128)S(1)}, u32[]{:S(2)}, u32[]{:S(2)}) collective-permute-start(f32[16]{0:T(128)S(1)} %fusion.46), channel_id=1, source_target_pairs={{0,8},{4,12},{8,0},{12,4},{16,24},{20,28},{24,16},{28,20},{1,9},{5... | collective-permute-start | bytes 200 | tf_op jit(solution)/shard_map/ppermute | solution.py:18
  23.5 42.2 %copy-start.3 = (bf16[256,128]{1,0:T(8,128)(2,1)S(1)}, bf16[256,128]{1,0:T(8,128)(2,1)}, u32[]{:S(2)}) copy-start(bf16[256,128]{1,0:T(8,128)(2,1)} %param.16) | copy-start | bytes 196612
  65.9 4.1 %collective-permute-start = (bf16[16,64,128]{2,1,0:T(8,128)(2,1)S(1)}, bf16[16,64,128]{2,1,0:T(8,128)(2,1)S(1)}, u32[]{:S(2)}, u32[]{:S(2)}) collective-permute-start(bf16[16,64,128]{2,1,0:T(8,128)(2,1)S(1)} %get-tuple-element.48), channel_id=1, source_target_pairs={{0,4},{4,0},{8,12},{12,8},{16,20},{20,16},{24,28},{28,24},{1,5},{5... | collective-permute-start | bytes 786440 | tf_op jit(solution)/shard_map/ppermute | solution.py:19
  66.0 5.8 %copy-start.8 = (f32[16,256]{1,0:T(8,128)S(1)}, f32[16,256]{1,0:T(8,128)}, u32[]{:S(2)}) copy-start(f32[16,256]{1,0:T(8,128)} %copy-done.7) | copy-start | bytes 49156
  66.1 5.8 %copy-start.9 = (pred[256,256]{1,0:T(8,128)(4,1)S(1)}, pred[256,256]{1,0:T(8,128)(4,1)}, u32[]{:S(2)}) copy-start(pred[256,256]{1,0:T(8,128)(4,1)} %iota_compare_fusion) | copy-start | bytes 196612
  70.1 9.0 %copy-start.24 = (f32[16]{0:T(128)S(1)}, f32[16]{0:T(128)}, u32[]{:S(2)}) copy-start(f32[16]{0:T(128)} %copy-done.23) | copy-start | bytes 196
  70.1 9.0 %copy-start.28 = (f32[16]{0:T(128)S(1)}, f32[16]{0:T(128)}, u32[]{:S(2)}) copy-start(f32[16]{0:T(128)} %copy-done.27) | copy-start | bytes 196
  70.3 10.7 %copy-start.1 = (bf16[1,1024,128]{2,1,0:T(8,128)(2,1)S(1)}, bf16[1,1024,128]{2,1,0:T(8,128)(2,1)}, u32[]{:S(2)}) copy-start(bf16[1,1024,128]{2,1,0:T(8,128)(2,1)} %param.21) | copy-start | bytes 786436
  70.3 17.0 %copy-start.11 = (f32[256,16]{0,1:T(8,128)S(1)}, f32[256,16]{0,1:T(8,128)}, u32[]{:S(2)}) copy-start(f32[256,16]{0,1:T(8,128)} %copy.99) | copy-start | bytes 49156
  70.3 17.0 %copy-start.17 = (f32[16]{0:T(128)S(1)}, f32[16]{0:T(128)}, u32[]{:S(2)}) copy-start(f32[16]{0:T(128)} %get-tuple-element.35) | copy-start | bytes 196
  70.3 17.0 %copy-start.18 = (f32[16]{0:T(128)S(1)}, f32[16]{0:T(128)}, u32[]{:S(2)}) copy-start(f32[16]{0:T(128)} %get-tuple-element.36) | copy-start | bytes 196
  70.3 8.8 %collective-permute-start.2 = (bf16[16,64,128]{2,1,0:T(8,128)(2,1)S(1)}, bf16[16,64,128]{2,1,0:T(8,128)(2,1)S(1)}, u32[]{:S(2)}, u32[]{:S(2)}) collective-permute-start(bf16[16,64,128]{2,1,0:T(8,128)(2,1)S(1)} %fusion.48), channel_id=1, source_target_pairs={{0,8},{4,12},{8,0},{12,4},{16,24},{20,28},{24,16},{28,20},{1,9},{5... | collective-permute-start | bytes 786440 | tf_op jit(solution)/shard_map/ppermute | solution.py:19
  75.1 13.8 %copy-start.10 = (f32[256,16]{0,1:T(8,128)S(1)}, f32[256,16]{0,1:T(8,128)}, u32[]{:S(2)}) copy-start(f32[256,16]{0,1:T(8,128)} %copy.114) | copy-start | bytes 49156
  79.1 12.4 %copy-start.2 = (bf16[16,64,128]{2,1,0:T(8,128)(2,1)}, bf16[16,64,128]{2,1,0:T(8,128)(2,1)S(1)}, u32[]{:S(2)}) copy-start(bf16[16,64,128]{2,1,0:T(8,128)(2,1)S(1)} %collective-permute-done.2) | copy-start | bytes 786436
  79.4 7.9 %collective-permute-start.4 = (bf16[16,64,128]{2,1,0:T(8,128)(2,1)S(1)}, bf16[16,64,128]{2,1,0:T(8,128)(2,1)S(1)}, u32[]{:S(2)}, u32[]{:S(2)}) collective-permute-start(bf16[16,64,128]{2,1,0:T(8,128)(2,1)S(1)} %fusion.24), channel_id=1, source_target_pairs={{0,16},{4,20},{8,24},{12,28},{16,0},{20,4},{24,8},{28,12},{1,17},{... | collective-permute-start | bytes 786440 | tf_op jit(solution)/shard_map/ppermute | solution.py:19
  87.3 10.0 %copy-start.5 = (bf16[16,64,128]{2,1,0:T(8,128)(2,1)}, bf16[16,64,128]{2,1,0:T(8,128)(2,1)S(1)}, u32[]{:S(2)}) copy-start(bf16[16,64,128]{2,1,0:T(8,128)(2,1)S(1)} %collective-permute-done.4) | copy-start | bytes 786436
  103.0 6.6 %copy-start.13 = (f32[16,256]{1,0:T(8,128)S(1)}, f32[16,256]{1,0:T(8,128)}, u32[]{:S(2)}) copy-start(f32[16,256]{1,0:T(8,128)} %get-tuple-element.29) | copy-start | bytes 49156
  106.6 5.6 %copy-start.14 = (f32[16]{0:T(128)S(1)}, f32[16]{0:T(128)}, u32[]{:S(2)}) copy-start(f32[16]{0:T(128)} %param.18) | copy-start | bytes 196
  106.6 5.6 %copy-start.22 = (f32[16]{0:T(128)S(1)}, f32[16]{0:T(128)}, u32[]{:S(2)}) copy-start(f32[16]{0:T(128)} %copy-done.21) | copy-start | bytes 196
  106.6 7.0 %copy-start.12 = (f32[256,16]{0,1:T(8,128)S(1)}, f32[256,16]{0,1:T(8,128)}, u32[]{:S(2)}) copy-start(f32[256,16]{0,1:T(8,128)} %get-tuple-element.32) | copy-start | bytes 49156
  106.6 7.2 %copy-start.26 = (f32[16]{0:T(128)S(1)}, f32[16]{0:T(128)}, u32[]{:S(2)}) copy-start(f32[16]{0:T(128)} %copy-done.25) | copy-start | bytes 196
  113.9 1.2 collective-permute-start.5
  115.1 3.7 %collective-permute-start.6 = (f32[3,16]{1,0:T(4,128)S(1)}, f32[3,16]{1,0:T(4,128)S(1)}, u32[]{:S(2)}, u32[]{:S(2)}) collective-permute-start(f32[3,16]{1,0:T(4,128)S(1)} %fusion.47), channel_id=1, source_target_pairs={{0,8},{4,12},{8,0},{12,4},{16,24},{20,28},{24,16},{28,20},{1,9},{5... | collective-permute-start | bytes 584 | tf_op jit(solution)/shard_map/ppermute | solution.py:37
  118.8 3.7 %collective-permute-start.7 = (f32[3,16]{1,0:T(4,128)S(1)}, f32[3,16]{1,0:T(4,128)S(1)}, u32[]{:S(2)}, u32[]{:S(2)}) collective-permute-start(f32[3,16]{1,0:T(4,128)S(1)} %fusion.69), channel_id=1, source_target_pairs={{0,16},{4,20},{8,24},{12,28},{16,0},{20,4},{24,8},{28,12},{1,17},{... | collective-permute-start | bytes 584 | tf_op jit(solution)/shard_map/ppermute | solution.py:37
  (7 other events, 18.1 us)
Sparse Core Ops, SparseCore 0:
  9.6 48.3 all-gather.1
  106.7 44.4 reduce-scatter.1

commit v2 on v1

--- a/solution.py
+++ b/solution.py
@@ -1,6 +1,10 @@
+import functools
+
 import jax
 import jax.numpy as jnp
 from jax import lax
+from jax.experimental import pallas as pl
+from jax.experimental.pallas import tpu as pltpu
 from jax.sharding import PartitionSpec as P
 
 
@@ -30,13 +34,248 @@
     return carried
 
 
-def summed(value, axis):
-    count = lax.axis_size(axis)
-    distance = 1
-    while distance < count:
-        value = value + lax.ppermute(value, axis, partners(count, distance))
-        distance *= 2
-    return value
+LAST = (((1,), (1,)), ((), ()))
+MESH = pl.DeviceIdType.MESH
+
+
+def tile_of(extent):
+    return 256 if extent % 256 == 0 else extent
+
+
+def ring_copy(src, dst, sems, way, step, target):
+    return pltpu.make_async_remote_copy(
+        src_ref=src,
+        dst_ref=dst,
+        send_sem=sems[0].at[way, step],
+        recv_sem=sems[1].at[way, step],
+        device_id={"head": target},
+        device_id_type=MESH,
+    )
+
+
+def gather_matmul_kernel(n, x_ref, w_hbm, o_ref, held, w_ref, total, send_sem, recv_sem, w_sem):
+    me = lax.axis_index("head")
+    right, left = (lax.rem(me + 1, n), lax.rem(me + n - 1, n))
+    tokens, depth = x_ref.shape
+    half = tokens // 2
+    width = o_ref.shape[1]
+    tile = tile_of(width)
+
+    def columns(offset):
+        owner = lax.rem(me + offset, n)
+        return pl.ds(pl.multiple_of(owner * depth, depth), depth)
+
+    def w_copy(offset):
+        where = columns(offset)
+        return pltpu.make_async_copy(w_hbm.at[:, where], w_ref.at[:, where], w_sem.at[offset])
+
+    barrier = pltpu.get_barrier_semaphore()
+    for neighbour in (left, right):
+        pl.semaphore_signal(barrier, inc=1, device_id={"head": neighbour}, device_id_type=MESH)
+    pl.semaphore_wait(barrier, 2)
+    sems = (send_sem, recv_sem)
+    order = []
+    for step in range(n):
+        for offset in ((n - step) % n, step):
+            if offset not in order:
+                order.append(offset)
+    loaded = set()
+    sent = []
+    for step in range(n):
+        sources = []
+        for way, target in ((0, right), (1, left)):
+            rows = pl.ds(way * half, half)
+            source = x_ref.at[rows] if step == 0 else held.at[step - 1, rows]
+            sources.append(source)
+            if step > 0:
+                sent[2 * (step - 1) + way].wait_recv()
+            if step < n - 1:
+                copy = ring_copy(source, held.at[step, rows], sems, way, step, target)
+                copy.start()
+                sent.append(copy)
+        if step == 0:
+            for offset in order:
+                w_copy(offset).start()
+        for way in (0, 1):
+            offset = (n - step) % n if way == 0 else step
+            if offset not in loaded:
+                w_copy(offset).wait()
+                loaded.add(offset)
+            where = columns(offset)
+            rows = pl.ds(way * half, half)
+            source = sources[way]
+
+            def multiply(index, carry):
+                outs = pl.ds(pl.multiple_of(index * tile, tile), tile)
+                part = lax.dot_general(
+                    source[...], w_ref[outs, where], LAST, preferred_element_type=jnp.float32
+                )
+                if step > 0:
+                    part = part + total[rows, outs]
+                if step < n - 1:
+                    total[rows, outs] = part
+                else:
+                    o_ref[rows, outs] = part.astype(o_ref.dtype)
+                return carry
+
+            lax.fori_loop(0, width // tile, multiply, 0)
+    for copy in sent:
+        copy.wait_send()
+
+
+def gather_matmul(x, w):
+    n = lax.axis_size("head")
+    tokens, depth = x.shape
+    width = w.shape[0]
+    vmem = pl.BlockSpec(memory_space=pltpu.VMEM)
+    return pl.pallas_call(
+        functools.partial(gather_matmul_kernel, n),
+        out_shape=jax.ShapeDtypeStruct((tokens, width), jnp.bfloat16),
+        in_specs=[vmem, pl.BlockSpec(memory_space=pl.ANY)],
+        out_specs=vmem,
+        scratch_shapes=[
+            pltpu.VMEM((n - 1, tokens, depth), jnp.bfloat16),
+            pltpu.VMEM(w.shape, jnp.bfloat16),
+            pltpu.VMEM((tokens, width), jnp.float32),
+            pltpu.SemaphoreType.DMA((2, n - 1)),
+            pltpu.SemaphoreType.DMA((2, n - 1)),
+            pltpu.SemaphoreType.DMA((n,)),
+        ],
+        compiler_params=pltpu.CompilerParams(
+            collective_id=0, has_side_effects=True, vmem_limit_bytes=40 * 2**20
+        ),
+        name="gather_matmul",
+    )(x, w)
+
+
+def matmul_scatter_kernel(
+    n, s, w_hbm, x_ref, bc_ref, p_ref, o_ref, obc_ref, op_ref,
+    w_ref, going, coming, p_in, send_sem, recv_sem, w_sem, p_send, p_recv,
+):
+    me = lax.axis_index("head")
+    mine = lax.axis_index("seq")
+    right, left = (lax.rem(me + 1, n), lax.rem(me + n - 1, n))
+    rows_here = o_ref.shape[0]
+    half = rows_here // 2
+    bc_half = obc_ref.shape[0] // 2
+    tile = tile_of(half)
+
+    def owner_of(way, step):
+        return lax.rem(me + 2 * n - 1 - step, n) if way == 0 else lax.rem(me + 1 + step, n)
+
+    def w_copy(way, step):
+        start = pl.multiple_of(owner_of(way, step) * rows_here + way * half, half)
+        rows = pl.ds(start, half)
+        return pltpu.make_async_copy(w_hbm.at[rows], w_ref.at[rows], w_sem.at[way, step])
+
+    for step in range(n):
+        for way in (0, 1):
+            w_copy(way, step).start()
+    barrier = pltpu.get_barrier_semaphore()
+    for neighbour in (left, right):
+        pl.semaphore_signal(barrier, inc=1, device_id={"head": neighbour}, device_id_type=MESH)
+    for away in range(1, s):
+        pl.semaphore_signal(
+            barrier, inc=1, device_id={"seq": lax.rem(mine + away, s)}, device_id_type=MESH
+        )
+    pl.semaphore_wait(barrier, 2 + s - 1)
+    sems = (send_sem, recv_sem)
+    p_copies = []
+    for away in range(1, s):
+        copy = pltpu.make_async_remote_copy(
+            src_ref=p_ref,
+            dst_ref=p_in.at[away - 1],
+            send_sem=p_send.at[away - 1],
+            recv_sem=p_recv.at[away - 1],
+            device_id={"seq": lax.rem(mine + away, s)},
+            device_id_type=MESH,
+        )
+        p_copies.append(copy)
+    sent = []
+    for step in range(n):
+        now = []
+        for way, target in ((0, right), (1, left)):
+            owner = owner_of(way, step)
+            w_copy(way, step).wait()
+            if step > 0:
+                sent[2 * (step - 1) + way].wait_recv()
+            first = pl.multiple_of(owner * rows_here + way * half, half)
+
+            def finish(start, count, part, target_ref, base):
+                if step > 0:
+                    old = coming[way, step - 1, pl.ds(start, count), :]
+                    part = part.astype(jnp.bfloat16).astype(jnp.float32) + old.astype(jnp.float32)
+                if step < n - 1:
+                    going[way, step, pl.ds(start, count), :] = part.astype(jnp.bfloat16)
+                else:
+                    target_ref[pl.ds(base, count), :] = part.astype(jnp.bfloat16)
+
+            def multiply(index, carry):
+                start = pl.multiple_of(index * tile, tile)
+                part = lax.dot_general(
+                    w_ref[pl.ds(first + start, tile), :],
+                    x_ref[...],
+                    LAST,
+                    preferred_element_type=jnp.float32,
+                )
+                base = pl.multiple_of(way * half + start, tile)
+                finish(start, tile, part, o_ref, base)
+                return carry
+
+            lax.fori_loop(0, half // tile, multiply, 0)
+            bc_start = pl.multiple_of(owner * 2 * bc_half + way * bc_half, bc_half)
+            finish(half, bc_half, bc_ref[pl.ds(bc_start, bc_half), :], obc_ref, way * bc_half)
+            if step < n - 1:
+                copy = ring_copy(
+                    going.at[way, step], coming.at[way, step], sems, way, step, target
+                )
+                copy.start()
+                sent.append(copy)
+        if step == 0:
+            for copy in p_copies:
+                copy.start()
+    value = p_ref[...]
+    for index, copy in enumerate(p_copies):
+        copy.wait_recv()
+        value = value + p_in[index]
+    op_ref[...] = value
+    for copy in p_copies + sent:
+        copy.wait_send()
+
+
+def matmul_scatter(w, x, bc, params):
+    n, s = (lax.axis_size("head"), lax.axis_size("seq"))
+    tokens = x.shape[0]
+    rows_here, bc_here = (w.shape[0] // n, bc.shape[0] // n)
+    padded = jnp.zeros((8, 128), jnp.float32).at[: params.shape[0], : params.shape[1]].set(params)
+    vmem = pl.BlockSpec(memory_space=pltpu.VMEM)
+    packet = (2, n - 1, (rows_here + bc_here) // 2, tokens)
+    in_sum, bc_sum, param_sum = pl.pallas_call(
+        functools.partial(matmul_scatter_kernel, n, s),
+        out_shape=(
+            jax.ShapeDtypeStruct((rows_here, tokens), jnp.bfloat16),
+            jax.ShapeDtypeStruct((bc_here, tokens), jnp.bfloat16),
+            jax.ShapeDtypeStruct((8, 128), jnp.float32),
+        ),
+        in_specs=[pl.BlockSpec(memory_space=pl.ANY), vmem, vmem, vmem],
+        out_specs=(vmem, vmem, vmem),
+        scratch_shapes=[
+            pltpu.VMEM(w.shape, jnp.bfloat16),
+            pltpu.VMEM(packet, jnp.bfloat16),
+            pltpu.VMEM(packet, jnp.bfloat16),
+            pltpu.VMEM((s - 1, 8, 128), jnp.float32),
+            pltpu.SemaphoreType.DMA((2, n - 1)),
+            pltpu.SemaphoreType.DMA((2, n - 1)),
+            pltpu.SemaphoreType.DMA((2, n)),
+            pltpu.SemaphoreType.DMA((s - 1,)),
+            pltpu.SemaphoreType.DMA((s - 1,)),
+        ],
+        compiler_params=pltpu.CompilerParams(
+            collective_id=1, has_side_effects=True, vmem_limit_bytes=40 * 2**20
+        ),
+        name="matmul_scatter",
+    )(w, x, bc, padded)
+    return in_sum, bc_sum, param_sum[: params.shape[0], : params.shape[1]]
 
 
 def shards(out_grad, x_in, b_in, c_in, dt_raw, dt_bias, a_log, d_skip, states, w_out, w_in):
@@ -45,13 +284,8 @@
     head_dim = inner_here // group_heads
     state_dim = b_in.shape[1]
     contract_last = (((1,), (1,)), ((), ()))
-    head_sum = lax.dot_general(
-        lax.all_gather(out_grad, "head", axis=1, tiled=True),
-        w_out,
-        contract_last,
-        preferred_element_type=jnp.float32,
-    )
-    dy_heads = head_sum.astype(jnp.bfloat16).reshape(tokens_here, group_heads, head_dim)
+    head_grad = gather_matmul(out_grad, w_out)
+    dy_heads = head_grad.reshape(tokens_here, group_heads, head_dim)
     dy_wide = dy_heads.astype(jnp.float32)
     x_heads = x_in.reshape(tokens_here, group_heads, head_dim)
     x_wide = x_heads.astype(jnp.float32)
@@ -115,24 +349,9 @@
     param_terms = jnp.stack(
         [jnp.sum(step_grad * log_step, axis=1), skip_terms, jnp.sum(dt_grad, axis=1)]
     )
-    heads_count = lax.axis_size("head")
-    in_term = lax.dot_general(
-        w_in, x_grad, contract_last, preferred_element_type=jnp.float32
-    ).astype(jnp.bfloat16)
-    rows_here = in_term.shape[0] // heads_count
-    both = jnp.concatenate(
-        [
-            in_term.reshape(heads_count, rows_here, tokens_here),
-            bc_part.astype(jnp.bfloat16).reshape(heads_count, -1, tokens_here),
-        ],
-        axis=1,
-    )
-    both_sum = lax.psum_scatter(
-        both.reshape(-1, tokens_here), "head", scatter_dimension=0, tiled=True
-    )
-    in_part, bc_sum = (both_sum[:rows_here], both_sum[rows_here:])
+    in_part, bc_sum, param_sum = matmul_scatter(w_in, x_grad, bc_part, param_terms)
     norm_scale = (lax.axis_size("seq") * tokens_here * head_dim) ** (-0.5)
-    param_grad = summed(param_terms, "seq") * norm_scale
+    param_grad = param_sum * norm_scale
     return (in_part, bc_sum, dt_grad, param_grad)
 
 

time: 162 us -> 150 us (0.926)
  Pallas kernels: 0 us -> 87.7 us
  waiting for transfers between devices: 78.4 us -> 8.47 us
  between operations: 14.4 us -> 1.01 us
  matrix products: 26.6 us -> 15.4 us
  starting transfers between devices: 9.59 us -> 4.07 us
  other arithmetic: 10.9 us -> 14.2 us
  local copies, waits for them, and re-layouts: 21.4 us -> 18.3 us
    pallas_call x0 -> x2, Pallas kernels: none -> 87.7 us  [the longest x1 45.1 us: matmul_scatter(): pl.pallas_call(functools.partial(matmul_scatter_kernel, n, s), out_shape=...]
    all_gather x1 -> x0, waiting for transfers between devices: 34.5 us -> none  [shards(): lax.all_gather(out_grad, 'head', axis=1, tiled=True)]
    reduce_scatter x1 -> x0, waiting for transfers between devices: 28.2 us -> none  [shards(): lax.psum_scatter(both.reshape(-1, tokens_here), 'head', scatter_dimension...]
    dot_general x2 -> x0, matrix products: 13 us -> none  [the longest x1 7.21 us: shards(): lax.dot_general(lax.all_gather(out_grad, 'head', axis=1, tiled=True), w_o...]
    unnamed x60 -> x50, local copies, waits for them, and re-layouts: 2.2 us -> 10.8 us
    ppermute x3, waiting for transfers between devices: 9.91 us -> 2.98 us  [entering(): lax.ppermute(state.astype(jnp.bfloat16), axis, pairs).astype(jnp.float32)]
    ppermute x2, waiting for transfers between devices: 0.15 us -> 5.49 us  [entering(): other_decay = lax.ppermute(decay, axis, pairs)]
    ppermute x3 -> x0, waiting for transfers between devices: 4.97 us -> none  [summed(): value = value + lax.ppermute(value, axis, partners(count, distance))]
  transfers between devices with their start and end apart: 10 -> 5, of which waited for: 8 -> 2; matrix products, arithmetic and copies ran while one was open for 17% -> 15% of each run, Pallas kernels for 0% -> 29%
where the time goes in v2:
time: 150 us; the launch traced here: 149 us
  Pallas kernels  87.7 us (58%)
  local copies, waits for them, and re-layouts  18.3 us (12%)
  matrix products  15.4 us (10%)
  other arithmetic  14.2 us (9%)
  waiting for transfers between devices  8.47 us (6%)
  starting transfers between devices  4.07 us (3%)
    pallas_call x1, Pallas kernels, matmul_scatter(): pl.pallas_call(functools.partial(matmul_scatter_kernel, n, s), out_shape=...  45.1 us
    pallas_call x1, Pallas kernels, gather_matmul(): pl.pallas_call(functools.partial(gather_matmul_kernel, n), out_shape=jax....  42.6 us
    unnamed x50, local copies, waits for them, and re-layouts  10.8 us
    ppermute x2, waiting for transfers between devices, entering(): other_decay = lax.ppermute(decay, axis, pairs)  5.49 us
    dot_general x1, matrix products, shards(): jnp.einsum('ihp,jhp->hij', dy_heads, x_scaled, preferred_element_type=jnp...  4.31 us
    convert_element_type x2, other arithmetic, entering(): state.astype(jnp.bfloat16)  3.82 us
    ppermute x3, starting transfers between devices, entering(): lax.ppermute(state.astype(jnp.bfloat16), axis, pairs).astype(jnp.float32)  3.04 us
  transfers between devices with their start and end apart: 5, of which 2 were waited for; matrix products, arithmetic and copies ran while one was open for 15% of the time, Pallas kernels for 29%

profile of v2, /device:TPU:0, one launch (start us, length us, event | category | flops | bytes accessed | tf_op | source)
XLA Modules:
  0.0 149.3 jit_solution(11654844929022754174)
XLA Ops:
  0.6 0.7 exponential_negate_fusion
  1.3 0.8 copy.87
  2.2 0.7 broadcast_multiply_fusion
  5.0 3.4 %copy-done.1 = bf16[1024,4096]{1,0:T(8,128)(2,1)S(1)} copy-done((bf16[1024,4096]{1,0:T(8,128)(2,1)S(1)}, bf16[1024,4096]{1,0:T(8,128)(2,1)}, u32[]{:S(2)}) %copy-start.1) | copy-done | bytes 8388632
  8.4 1.0 copy-done.3
  9.4 42.6 %gather_matmul.1 = bf16[256,1024]{1,0:T(8,128)(2,1)S(1)} custom-call(bf16[256,1024]{1,0:T(8,128)(2,1)S(1)} %copy-done.3, bf16[1024,4096]{1,0:T(8,128)(2,1)S(1)} %copy-done.1), custom_call_target="tpu_custom_call" | custom-call | tf_op jit(solution)/shard_map/gather_matmul/pallas_call | solution.py:131
  52.3 0.9 fusion.33
  53.2 1.0 fusion.48
  54.9 0.9 fusion.49
  55.8 0.7 copy.88
  56.9 2.3 %copy.97 = f32[256,1024]{0,1:T(8,128)} copy(bf16[256,1024]{1,0:T(8,128)(2,1)} %param.16) | data formatting | bytes 1572864 | tf_op jit(solution)/shard_map/convert_element_type | solution.py:291
  59.2 1.9 %fusion.13 = (f32[1024]{0:T(1024)}, bf16[256,1024]{1,0:T(8,128)(2,1)S(1)}) fusion(bf16[256,1024]{1,0:T(8,128)(2,1)S(1)} %gather_matmul.1, bf16[256,1024]{1,0:T(8,128)(2,1)} %param.16, f32[256,1024]{1,0:T(8,128)S(1)} %copy.98), kind=kLoop, calls=%fused_computation.28 | loop fusion | flops 1571840 | bytes 2625536 | tf_op jit(solution)/shard_map/reduce_sum | solution.py:318
  61.3 1.2 convolution_bitcast_fusion.1
  62.6 4.3 %fusion = (f32[16,256]{1,0:T(8,128)}, f32[16,256]{1,0:T(8,128)}, bf16[256,256]{1,0:T(8,128)(2,1)S(1)}) fusion(f32[16,256]{1,0:T(8,128)S(1)} %copy_bitcast_fusion, f32[256,256]{1,0:T(8,128)} %fusion.49, pred[256,256]{1,0:T(8,128)(4,1)} %iota_compare_fusion, bf16[256,16,64]{0,2,1:T(8,128)(2,1)S(1)} %bitcast.99, f32[256,16,64]{0,2,1:T(8,128)} %bitcast.105, ...), kind=kOutput, calls=%fused_computation.5 | convolution fusion | flops 146202624 | bytes 2097152 | tf_op jit(solution)/shard_map/ihp,jhp->hij/dot_general | solution.py:303
  66.9 2.3 %fusion.8 = f32[256,16,64]{0,2,1:T(8,128)} fusion(bf16[256,16,64]{0,2,1:T(8,128)(2,1)S(1)} %bitcast.100, f32[16,256]{1,0:T(8,128)S(1)} %copy_bitcast_fusion, f32[256,256]{1,0:T(8,128)S(1)} %copy-done.13, pred[256,256]{1,0:T(8,128)(4,1)S(1)} %copy-done.14), kind=kOutput, calls=%fused_computation.16 | convolution fusion | flops 139460608 | bytes 1916928 | tf_op jit(solution)/shard_map/hij,ihp->jhp/dot_general | solution.py:305
  69.2 1.9 %fusion.44 = bf16[16,64,128]{2,1,0:T(8,128)(2,1)} fusion(f32[16,64,128]{2,1,0:T(8,128)S(1)} %get-tuple-element.66, f32[16]{0:T(128)} %collective-permute-done.1, bf16[16,64,128]{2,1,0:T(8,128)(2,1)} %collective-permute-done, f32[16]{0:T(128)} %fusion.42, pred[]{:T(512)S(6)} %eq.15), kind=kLoop, calls=%fused_computation.97 | loop fusion | flops 917504 | bytes 1048705 | tf_op jit(solution)/shard_map/convert_element_type | solution.py:23
  71.0 1.5 collective-permute-start.2
  72.5 0.9 fusion.11
  74.5 5.5 %collective-permute-done.3 = f32[16]{0:T(128)S(1)} collective-permute-done((f32[16]{0:T(128)S(1)}, f32[16]{0:T(128)S(1)}, u32[]{:S(2)}, u32[]{:S(2)}) %collective-permute-start.3) | collective-permute-done | bytes 96 | tf_op jit(solution)/shard_map/ppermute | solution.py:22
  80.0 2.0 %fusion.21 = bf16[16,64,128]{2,1,0:T(8,128)(2,1)} fusion(bf16[16,64,128]{2,1,0:T(8,128)(2,1)S(1)} %collective-permute-done.2, f32[16]{0:T(128)S(1)} %collective-permute-done.3, f32[16]{0:T(128)S(1)} %fusion.43, pred[]{:T(512)S(6)} %eq.14, f32[16,64,128]{2,1,0:T(8,128)S(1)} %get-tuple-element.66, f32[16]{0:T(128)} %collective-permute-done.1, ...), kind=kLoop, calls=%fused_computation.48 | loop fusion | flops 1703936 | bytes 1310978 | tf_op jit(solution)/shard_map/convert_element_type | solution.py:23
  82.0 1.5 %collective-permute-start.4 = (bf16[16,64,128]{2,1,0:T(8,128)(2,1)}, bf16[16,64,128]{2,1,0:T(8,128)(2,1)}, u32[]{:S(2)}, u32[]{:S(2)}) collective-permute-start(bf16[16,64,128]{2,1,0:T(8,128)(2,1)} %fusion.21), channel_id=1, source_target_pairs={{0,16},{4,20},{8,24},{12,28},{16,0},{20,4},{24,8},{28,12},{1,17},{... | collective-permute-start | bytes 786440 | tf_op jit(solution)/shard_map/ppermute | solution.py:23
  84.8 0.8 copy.101
  85.6 0.8 copy.100
  87.1 3.0 %collective-permute-done.4 = bf16[16,64,128]{2,1,0:T(8,128)(2,1)} collective-permute-done((bf16[16,64,128]{2,1,0:T(8,128)(2,1)}, bf16[16,64,128]{2,1,0:T(8,128)(2,1)}, u32[]{:S(2)}, u32[]{:S(2)}) %collective-permute-start.4) | collective-permute-done | bytes 262176 | tf_op jit(solution)/shard_map/ppermute | solution.py:23
  90.1 1.5 convolution_bitcast_fusion.2
  91.5 0.9 fusion.10
  92.4 2.2 %multiply_reduce_fusion.1 = (f32[256,16]{0,1:T(8,128)S(1)}, f32[256,16]{0,1:T(8,128)S(1)}, bf16[256,16,64]{0,2,1:T(8,128)(2,1)S(1)}) fusion(f32[256,1024]{0,1:T(8,128)S(1)} %copy-done.7, f32[256,16,64]{0,2,1:T(8,128)} %fusion.8, f32[256,16]{0,1:T(8,128)S(1)} %copy.107, bf16[256,1024]{0,1:T(8,128)(2,1)S(1)} %copy-done.5, f32[16]{0:T(128)} %param.22, ...), kind=kOutput, calls=%fused_computation.33 | convolution fusion | flops 71950336 | bytes 4079811 | tf_op jit(solution)/shard_map/jn,hpn->jhp/dot_general | solution.py:322
  94.9 1.4 multiply_reduce_fusion.2
  97.8 0.7 copy.110
  98.8 3.4 %copy-done.2 = bf16[4096,1024]{1,0:T(8,128)(2,1)S(1)} copy-done((bf16[4096,1024]{1,0:T(8,128)(2,1)S(1)}, bf16[4096,1024]{1,0:T(8,128)(2,1)}, u32[]{:S(2)}) %copy-start.2) | copy-done | bytes 8388632
  102.2 45.1 %matmul_scatter.1 = (bf16[1024,256]{1,0:T(8,128)(2,1)S(1)}, bf16[64,256]{1,0:T(8,128)(2,1)S(1)}, f32[8,128]{1,0:T(8,128)S(1)}) custom-call(bf16[4096,1024]{1,0:T(8,128)(2,1)S(1)} %copy-done.2, bf16[256,1024]{1,0:T(8,128)(2,1)S(1)} %copy.109.x_ref, f32[256,256]{1,0:T(8,128)S(1)} %pad_maximum_fusion.bc_ref, f32[8,128]{1,0:T(8,128)S(1)} %select_maximum_fusion.p_ref), custom_call_target="tpu_custom_call" | custom-call | tf_op jit(solution)/shard_map/matmul_scatter/pallas_call | solution.py:253
  147.9 0.8 copy.118
  (92 shorter events, 9.9 us)
Async XLA Ops:
  0.6 54.3 %copy-start = (bf16[256,128]{1,0:T(8,128)(2,1)S(1)}, bf16[256,128]{1,0:T(8,128)(2,1)}, u32[]{:S(2)}) copy-start(bf16[256,128]{1,0:T(8,128)(2,1)} %param.17) | copy-start | bytes 196612
  1.3 1.6 %copy-start.21 = (f32[16]{0:T(128)}, f32[16]{0:T(128)S(1)}, u32[]{:S(2)}) copy-start(f32[16]{0:T(128)S(1)} %exponential_negate_fusion) | copy-start | bytes 196
  4.5 64.7 %collective-permute-start.1 = (f32[16]{0:T(128)}, f32[16]{0:T(128)}, u32[]{:S(2)}, u32[]{:S(2)}) collective-permute-start(f32[16]{0:T(128)} %fusion.42), channel_id=1, source_target_pairs={{0,4},{4,0},{8,12},{12,8},{16,20},{20,16},{24,28},{28,24},{1,5},{5... | collective-permute-start | bytes 200 | tf_op jit(solution)/shard_map/ppermute | solution.py:22
  5.0 3.4 %copy-start.1 = (bf16[1024,4096]{1,0:T(8,128)(2,1)S(1)}, bf16[1024,4096]{1,0:T(8,128)(2,1)}, u32[]{:S(2)}) copy-start(bf16[1024,4096]{1,0:T(8,128)(2,1)} %w_hbm.2) | copy-start | bytes 25165828
  8.4 1.0 copy-start.3
  9.4 42.9 %copy-start.18 = (f32[16]{0:T(128)}, f32[16]{0:T(128)S(1)}, u32[]{:S(2)}) copy-start(f32[16]{0:T(128)S(1)} %slice_bitcast_fusion) | copy-start | bytes 196
  9.4 42.9 %copy-start.16 = (f32[16]{0:T(128)S(1)}, f32[16]{0:T(128)}, u32[]{:S(2)}) copy-start(f32[16]{0:T(128)} %param.20) | copy-start | bytes 196
  9.4 43.8 %copy-start.8 = (bf16[256,128]{1,0:T(8,128)(2,1)S(1)}, bf16[256,128]{1,0:T(8,128)(2,1)}, u32[]{:S(2)}) copy-start(bf16[256,128]{1,0:T(8,128)(2,1)} %param.18) | copy-start | bytes 196612
  52.3 4.3 %copy-start.4 = (bf16[256,1024]{0,1:T(8,128)(2,1)}, bf16[256,1024]{0,1:T(8,128)(2,1)S(1)}, u32[]{:S(2)}) copy-start(bf16[256,1024]{0,1:T(8,128)(2,1)S(1)} %copy.89) | copy-start | bytes 1572868
  54.2 15.0 %collective-permute-start = (bf16[16,64,128]{2,1,0:T(8,128)(2,1)}, bf16[16,64,128]{2,1,0:T(8,128)(2,1)}, u32[]{:S(2)}, u32[]{:S(2)}) collective-permute-start(bf16[16,64,128]{2,1,0:T(8,128)(2,1)} %get-tuple-element.65), channel_id=1, source_target_pairs={{0,4},{4,0},{8,12},{12,8},{16,20},{20,16},{24,28},{28,24},{1,5},{5... | collective-permute-start | bytes 786440 | tf_op jit(solution)/shard_map/ppermute | solution.py:23
  56.9 5.6 %copy-start.5 = (bf16[256,1024]{0,1:T(8,128)(2,1)S(1)}, bf16[256,1024]{0,1:T(8,128)(2,1)}, u32[]{:S(2)}) copy-start(bf16[256,1024]{0,1:T(8,128)(2,1)} %copy-done.4) | copy-start | bytes 1572868
  62.5 4.3 %copy-start.13 = (f32[256,256]{1,0:T(8,128)S(1)}, f32[256,256]{1,0:T(8,128)}, u32[]{:S(2)}) copy-start(f32[256,256]{1,0:T(8,128)} %fusion.49) | copy-start | bytes 786436
  62.5 4.3 %copy-start.14 = (pred[256,256]{1,0:T(8,128)(4,1)S(1)}, pred[256,256]{1,0:T(8,128)(4,1)}, u32[]{:S(2)}) copy-start(pred[256,256]{1,0:T(8,128)(4,1)} %iota_compare_fusion) | copy-start | bytes 196612
  66.9 16.6 %copy-start.6 = (bf16[1,1024,128]{2,1,0:T(8,128)(2,1)S(1)}, bf16[1,1024,128]{2,1,0:T(8,128)(2,1)}, u32[]{:S(2)}) copy-start(bf16[1,1024,128]{2,1,0:T(8,128)(2,1)} %param.23) | copy-start | bytes 786436
  66.9 17.1 %copy-start.12 = (f32[256,16]{1,0:T(8,128)S(1)}, f32[256,16]{1,0:T(8,128)}, u32[]{:S(2)}) copy-start(f32[256,16]{1,0:T(8,128)} %get-tuple-element.60) | copy-start | bytes 49156
  66.9 17.2 %copy-start.11 = (f32[256,16]{1,0:T(8,128)S(1)}, f32[256,16]{1,0:T(8,128)}, u32[]{:S(2)}) copy-start(f32[256,16]{1,0:T(8,128)} %get-tuple-element.61) | copy-start | bytes 49156
  66.9 23.2 %copy-start.7 = (f32[256,1024]{0,1:T(8,128)S(1)}, f32[256,1024]{0,1:T(8,128)}, u32[]{:S(2)}) copy-start(f32[256,1024]{0,1:T(8,128)} %copy.97) | copy-start | bytes 3145732
  69.2 14.9 %copy-start.15 = (f32[1024]{0:T(1024)S(1)}, f32[1024]{0:T(1024)}, u32[]{:S(2)}) copy-start(f32[1024]{0:T(1024)} %get-tuple-element.56) | copy-start | bytes 12292
  71.0 9.0 %collective-permute-start.2 = (bf16[16,64,128]{2,1,0:T(8,128)(2,1)}, bf16[16,64,128]{2,1,0:T(8,128)(2,1)S(1)}, u32[]{:S(2)}, u32[]{:S(2)}) collective-permute-start(bf16[16,64,128]{2,1,0:T(8,128)(2,1)} %fusion.44), channel_id=1, source_target_pairs={{0,8},{4,12},{8,0},{12,4},{16,24},{20,28},{24,16},{28,20},{1,9},{5... | collective-permute-start | bytes 786440 | tf_op jit(solution)/shard_map/ppermute | solution.py:23
  74.0 6.0 %collective-permute-start.3 = (f32[16]{0:T(128)S(1)}, f32[16]{0:T(128)S(1)}, u32[]{:S(2)}, u32[]{:S(2)}) collective-permute-start(f32[16]{0:T(128)S(1)} %fusion.43), channel_id=1, source_target_pairs={{0,8},{4,12},{8,0},{12,4},{16,24},{20,28},{24,16},{28,20},{1,9},{5... | collective-permute-start | bytes 200 | tf_op jit(solution)/shard_map/ppermute | solution.py:22
  82.0 8.1 %collective-permute-start.4 = (bf16[16,64,128]{2,1,0:T(8,128)(2,1)}, bf16[16,64,128]{2,1,0:T(8,128)(2,1)}, u32[]{:S(2)}, u32[]{:S(2)}) collective-permute-start(bf16[16,64,128]{2,1,0:T(8,128)(2,1)} %fusion.21), channel_id=1, source_target_pairs={{0,16},{4,20},{8,24},{12,28},{16,0},{20,4},{24,8},{28,12},{1,17},{... | collective-permute-start | bytes 786440 | tf_op jit(solution)/shard_map/ppermute | solution.py:23
  83.8 10.9 %copy-start.17 = (f32[16]{0:T(128)S(1)}, f32[16]{0:T(128)}, u32[]{:S(2)}) copy-start(f32[16]{0:T(128)} %param.20) | copy-start | bytes 196
  83.8 10.9 %copy-start.19 = (f32[16]{0:T(128)S(1)}, f32[16]{0:T(128)}, u32[]{:S(2)}) copy-start(f32[16]{0:T(128)} %copy-done.18) | copy-start | bytes 196
  92.4 5.2 %copy-start.22 = (f32[16]{0:T(128)S(1)}, f32[16]{0:T(128)}, u32[]{:S(2)}) copy-start(f32[16]{0:T(128)} %copy-done.21) | copy-start | bytes 196
  92.4 6.3 %copy-start.20 = (f32[16]{0:T(128)S(1)}, f32[16]{0:T(128)}, u32[]{:S(2)}) copy-start(f32[16]{0:T(128)} %reduce_sum.126) | copy-start | bytes 196
  94.6 4.1 %copy-start.9 = (f32[128,256]{1,0:T(8,128)S(1)}, f32[128,256]{1,0:T(8,128)}, u32[]{:S(2)}) copy-start(f32[128,256]{1,0:T(8,128)} %fusion.11) | copy-start | bytes 393220
  94.6 4.1 %copy-start.10 = (f32[128,256]{1,0:T(8,128)S(1)}, f32[128,256]{1,0:T(8,128)}, u32[]{:S(2)}) copy-start(f32[128,256]{1,0:T(8,128)} %fusion.10) | copy-start | bytes 393220
  98.8 3.4 %copy-start.2 = (bf16[4096,1024]{1,0:T(8,128)(2,1)S(1)}, bf16[4096,1024]{1,0:T(8,128)(2,1)}, u32[]{:S(2)}) copy-start(bf16[4096,1024]{1,0:T(8,128)(2,1)} %w_hbm.3) | copy-start | bytes 25165828

commit v3 on v2

--- a/solution.py
+++ b/solution.py
@@ -36,6 +36,7 @@
 
 LAST = (((1,), (1,)), ((), ()))
 MESH = pl.DeviceIdType.MESH
+CHUNKS = 2
 
 
 def tile_of(extent):
@@ -80,19 +81,19 @@
             if offset not in order:
                 order.append(offset)
     loaded = set()
-    sent = []
+    sent = {}
     for step in range(n):
-        sources = []
-        for way, target in ((0, right), (1, left)):
-            rows = pl.ds(way * half, half)
-            source = x_ref.at[rows] if step == 0 else held.at[step - 1, rows]
-            sources.append(source)
-            if step > 0:
-                sent[2 * (step - 1) + way].wait_recv()
-            if step < n - 1:
-                copy = ring_copy(source, held.at[step, rows], sems, way, step, target)
-                copy.start()
-                sent.append(copy)
+        for chunk in range(CHUNKS):
+            for way, target in ((0, right), (1, left)):
+                lane = way * CHUNKS + chunk
+                rows = pl.ds(lane * (half // CHUNKS), half // CHUNKS)
+                if step > 0:
+                    sent[step - 1, lane].wait_recv()
+                if step < n - 1:
+                    source = x_ref.at[rows] if step == 0 else held.at[step - 1, rows]
+                    copy = ring_copy(source, held.at[step, rows], sems, lane, step, target)
+                    copy.start()
+                    sent[step, lane] = copy
         if step == 0:
             for offset in order:
                 w_copy(offset).start()
@@ -103,7 +104,7 @@
                 loaded.add(offset)
             where = columns(offset)
             rows = pl.ds(way * half, half)
-            source = sources[way]
+            source = x_ref.at[rows] if step == 0 else held.at[step - 1, rows]
 
             def multiply(index, carry):
                 outs = pl.ds(pl.multiple_of(index * tile, tile), tile)
@@ -119,7 +120,7 @@
                 return carry
 
             lax.fori_loop(0, width // tile, multiply, 0)
-    for copy in sent:
+    for copy in sent.values():
         copy.wait_send()
 
 
@@ -137,12 +138,12 @@
             pltpu.VMEM((n - 1, tokens, depth), jnp.bfloat16),
             pltpu.VMEM(w.shape, jnp.bfloat16),
             pltpu.VMEM((tokens, width), jnp.float32),
-            pltpu.SemaphoreType.DMA((2, n - 1)),
-            pltpu.SemaphoreType.DMA((2, n - 1)),
+            pltpu.SemaphoreType.DMA((2 * CHUNKS, n - 1)),
+            pltpu.SemaphoreType.DMA((2 * CHUNKS, n - 1)),
             pltpu.SemaphoreType.DMA((n,)),
         ],
         compiler_params=pltpu.CompilerParams(
-            collective_id=0, has_side_effects=True, vmem_limit_bytes=40 * 2**20
+            collective_id=0, has_side_effects=True, vmem_limit_bytes=60 * 2**20
         ),
         name="gather_matmul",
     )(x, w)
@@ -158,7 +159,8 @@
     rows_here = o_ref.shape[0]
     half = rows_here // 2
     bc_half = obc_ref.shape[0] // 2
-    tile = tile_of(half)
+    piece = half // CHUNKS
+    tile = tile_of(piece)
 
     def owner_of(way, step):
         return lax.rem(me + 2 * n - 1 - step, n) if way == 0 else lax.rem(me + 1 + step, n)
@@ -191,14 +193,16 @@
             device_id_type=MESH,
         )
         p_copies.append(copy)
-    sent = []
+    sent = {}
     for step in range(n):
-        now = []
-        for way, target in ((0, right), (1, left)):
+        for chunk, way in ((c, w) for c in range(CHUNKS) for w in (0, 1)):
+            target = left if way else right
+            lane = way * CHUNKS + chunk
             owner = owner_of(way, step)
-            w_copy(way, step).wait()
+            if chunk == 0:
+                w_copy(way, step).wait()
             if step > 0:
-                sent[2 * (step - 1) + way].wait_recv()
+                sent[step - 1, lane].wait_recv()
             first = pl.multiple_of(owner * rows_here + way * half, half)
 
             def finish(start, count, part, target_ref, base):
@@ -211,7 +215,7 @@
                     target_ref[pl.ds(base, count), :] = part.astype(jnp.bfloat16)
 
             def multiply(index, carry):
-                start = pl.multiple_of(index * tile, tile)
+                start = pl.multiple_of(chunk * piece + index * tile, tile)
                 part = lax.dot_general(
                     w_ref[pl.ds(first + start, tile), :],
                     x_ref[...],
@@ -222,15 +226,19 @@
                 finish(start, tile, part, o_ref, base)
                 return carry
 
-            lax.fori_loop(0, half // tile, multiply, 0)
-            bc_start = pl.multiple_of(owner * 2 * bc_half + way * bc_half, bc_half)
-            finish(half, bc_half, bc_ref[pl.ds(bc_start, bc_half), :], obc_ref, way * bc_half)
+            lax.fori_loop(0, piece // tile, multiply, 0)
+            span = piece
+            if chunk == CHUNKS - 1:
+                span = piece + bc_half
+                bc_start = pl.multiple_of(owner * 2 * bc_half + way * bc_half, bc_half)
+                finish(half, bc_half, bc_ref[pl.ds(bc_start, bc_half), :], obc_ref, way * bc_half)
             if step < n - 1:
+                rows = pl.ds(chunk * piece, span)
                 copy = ring_copy(
-                    going.at[way, step], coming.at[way, step], sems, way, step, target
+                    going.at[way, step, rows], coming.at[way, step, rows], sems, lane, step, target
                 )
                 copy.start()
-                sent.append(copy)
+                sent[step, lane] = copy
         if step == 0:
             for copy in p_copies:
                 copy.start()
@@ -239,7 +247,7 @@
         copy.wait_recv()
         value = value + p_in[index]
     op_ref[...] = value
-    for copy in p_copies + sent:
+    for copy in p_copies + list(sent.values()):
         copy.wait_send()
 
 
@@ -264,14 +272,14 @@
             pltpu.VMEM(packet, jnp.bfloat16),
             pltpu.VMEM(packet, jnp.bfloat16),
             pltpu.VMEM((s - 1, 8, 128), jnp.float32),
-            pltpu.SemaphoreType.DMA((2, n - 1)),
-            pltpu.SemaphoreType.DMA((2, n - 1)),
+            pltpu.SemaphoreType.DMA((2 * CHUNKS, n - 1)),
+            pltpu.SemaphoreType.DMA((2 * CHUNKS, n - 1)),
             pltpu.SemaphoreType.DMA((2, n)),
             pltpu.SemaphoreType.DMA((s - 1,)),
             pltpu.SemaphoreType.DMA((s - 1,)),
         ],
         compiler_params=pltpu.CompilerParams(
-            collective_id=1, has_side_effects=True, vmem_limit_bytes=40 * 2**20
+            collective_id=1, has_side_effects=True, vmem_limit_bytes=60 * 2**20
         ),
         name="matmul_scatter",
     )(w, x, bc, padded)
@@ -286,7 +294,6 @@
     contract_last = (((1,), (1,)), ((), ()))
     head_grad = gather_matmul(out_grad, w_out)
     dy_heads = head_grad.reshape(tokens_here, group_heads, head_dim)
-    dy_wide = dy_heads.astype(jnp.float32)
     x_heads = x_in.reshape(tokens_here, group_heads, head_dim)
     x_wide = x_heads.astype(jnp.float32)
     decay_rate = jnp.exp(a_log)
@@ -297,6 +304,11 @@
     causal = positions[:, None] >= positions[None, :]
     log_gaps = cumlog[:, :, None] - cumlog[:, None, :]
     decay_mask = jnp.where(causal[None], jnp.exp(jnp.minimum(log_gaps, 0.0)), 0.0)
+    start_decay = jnp.exp(cumlog)
+    dy_decay = (dy_heads.astype(jnp.float32) * start_decay.T[:, :, None]).astype(jnp.bfloat16)
+    local_state = jnp.einsum("ihp,in->hpn", dy_decay, c_in, preferred_element_type=jnp.float32)
+    dy_heads, local_state = lax.optimization_barrier((dy_heads, local_state))
+    dy_wide = dy_heads.astype(jnp.float32)
     scores = lax.dot_general(c_in, b_in, contract_last, preferred_element_type=jnp.float32)
     step_rows = step_size.T
     x_scaled = (x_wide * step_rows[:, :, None]).astype(jnp.bfloat16)
@@ -304,9 +316,6 @@
     kernel = (scores[None] * decay_mask).astype(jnp.bfloat16)
     intra_back = jnp.einsum("hij,ihp->jhp", kernel, dy_heads, preferred_element_type=jnp.float32)
     masked_dots = (pair_dots * decay_mask).astype(jnp.bfloat16)
-    start_decay = jnp.exp(cumlog)
-    dy_decay = (dy_wide * start_decay.T[:, :, None]).astype(jnp.bfloat16)
-    local_state = jnp.einsum("ihp,in->hpn", dy_decay, c_in, preferred_element_type=jnp.float32)
     end_total = jnp.exp(cumlog[:, -1])
     entry_state = states.reshape(group_heads, head_dim, state_dim)
     db_intra = jnp.einsum("hij,in->nj", masked_dots, c_in, preferred_element_type=jnp.float32)

time: 150 us -> 147 us (0.980)
  local copies, waits for them, and re-layouts: 18.3 us -> 16.1 us
  matrix products: 15.4 us -> 13.9 us
    unnamed x50 -> x44, local copies, waits for them, and re-layouts: 10.8 us -> 4.83 us
    reduce_sum x2 -> x0, other arithmetic: 2.51 us -> none  [shards(): skip_terms = jnp.sum(dy_wide * x_wide, axis=(0, 2))]
    ppermute x3, waiting for transfers between devices: 2.98 us -> 0.87 us  [entering(): lax.ppermute(state.astype(jnp.bfloat16), axis, pairs).astype(jnp.float32)]
    transpose x1, local copies, waits for them, and re-layouts: 0.06 us -> 1.58 us  [shards(): end_decay.T[:, :, None] * state_back]
    convert_element_type x2 -> x3, other arithmetic: 3.82 us -> 4.58 us  [entering(): state.astype(jnp.bfloat16)]
  transfers between devices with their start and end apart: 5 -> 5, of which waited for: 2 -> 2; matrix products, arithmetic and copies ran while one was open for 15% -> 15% of each run, Pallas kernels for 29% -> 30%
where the time goes in v3:
time: 147 us; the launch traced here: 146 us
  Pallas kernels  88.7 us (60%)
  local copies, waits for them, and re-layouts  16.1 us (11%)
  other arithmetic  15.5 us (11%)
  matrix products  13.9 us (9%)
  waiting for transfers between devices  7.03 us (5%)
  starting transfers between devices  4.04 us (3%)
    pallas_call x1, Pallas kernels, matmul_scatter(): pl.pallas_call(functools.partial(matmul_scatter_kernel, n, s), out_shape=...  45.2 us
    pallas_call x1, Pallas kernels, gather_matmul(): pl.pallas_call(functools.partial(gather_matmul_kernel, n), out_shape=jax....  43.6 us
    ppermute x2, waiting for transfers between devices, entering(): other_decay = lax.ppermute(decay, axis, pairs)  6.16 us
    unnamed x44, local copies, waits for them, and re-layouts  4.83 us
    convert_element_type x3, other arithmetic, entering(): state.astype(jnp.bfloat16)  4.58 us
    dot_general x1, matrix products, shards(): jnp.einsum('ihp,jhp->hij', dy_heads, x_scaled, preferred_element_type=jnp...  4.1 us
    ppermute x3, starting transfers between devices, entering(): lax.ppermute(state.astype(jnp.bfloat16), axis, pairs).astype(jnp.float32)  3.01 us
  transfers between devices with their start and end apart: 5, of which 2 were waited for; matrix products, arithmetic and copies ran while one was open for 15% of the time, Pallas kernels for 30%

profile of v3, /device:TPU:0, one launch (start us, length us, event | category | flops | bytes accessed | tf_op | source)
XLA Modules:
  0.0 146.4 jit_solution(11278210356497153988)
XLA Ops:
  0.6 0.7 exponential_negate_fusion
  1.3 0.8 copy.74
  2.2 0.7 broadcast_multiply_fusion
  5.0 43.6 %gather_matmul.1 = bf16[256,1024]{1,0:T(8,128)(2,1)} custom-call(bf16[256,1024]{1,0:T(8,128)(2,1)} %x_ref.1, bf16[1024,4096]{1,0:T(8,128)(2,1)} %w_hbm.2), custom_call_target="tpu_custom_call" | custom-call | tf_op jit(solution)/shard_map/gather_matmul/pallas_call | solution.py:132
  48.6 1.3 copy.76
  49.9 0.9 fusion.30
  51.1 0.8 convert_element_type.69
  52.6 0.9 fusion.45
  54.9 1.2 copy.84
  56.2 1.9 %convolution_bitcast_fusion.1 = f32[256,128]{0,1:T(8,128)} fusion(bf16[256,16,64]{0,2,1:T(8,128)(2,1)S(1)} %bitcast.94, bf16[16,64,128]{2,1,0:T(8,128)(2,1)} %bitcast.100), kind=kOutput, calls=%fused_computation.19 | convolution fusion | flops 67108864 | bytes 917504 | tf_op jit(solution)/shard_map/ihp,hpn->ni/dot_general | solution.py:323
  58.1 4.1 %fusion = (f32[16,256]{1,0:T(8,128)}, f32[16,256]{1,0:T(8,128)}, bf16[256,256]{1,0:T(8,128)(2,1)S(1)}) fusion(f32[16,256]{1,0:T(8,128)S(1)} %copy_bitcast_fusion, f32[256,256]{1,0:T(8,128)} %fusion.45, pred[256,256]{1,0:T(8,128)(4,1)} %iota_compare_fusion, bf16[256,16,64]{0,2,1:T(8,128)(2,1)S(1)} %bitcast.96, f32[256,16,64]{0,2,1:T(8,128)S(1)} %bitcast.103, ...), kind=kOutput, calls=%fused_computation.5 | convolution fusion | flops 146202624 | bytes 2097152 | tf_op jit(solution)/shard_map/ihp,jhp->hij/dot_general | solution.py:315
  62.2 2.3 %fusion.8 = f32[256,16,64]{0,2,1:T(8,128)} fusion(bf16[256,16,64]{0,2,1:T(8,128)(2,1)S(1)} %bitcast.97, f32[16,256]{1,0:T(8,128)S(1)} %copy_bitcast_fusion, f32[256,256]{1,0:T(8,128)S(1)} %copy-done.9, pred[256,256]{1,0:T(8,128)(4,1)S(1)} %copy-done.10), kind=kOutput, calls=%fused_computation.16 | convolution fusion | flops 139460608 | bytes 1916928 | tf_op jit(solution)/shard_map/hij,ihp->jhp/dot_general | solution.py:317
  64.5 1.9 %fusion.41 = bf16[16,64,128]{2,1,0:T(8,128)(2,1)} fusion(f32[16,64,128]{2,1,0:T(8,128)S(1)} %fusion.20, f32[16]{0:T(128)} %collective-permute-done.1, bf16[16,64,128]{2,1,0:T(8,128)(2,1)} %collective-permute-done, f32[16]{0:T(128)} %fusion.39, pred[]{:T(512)S(6)} %eq.15), kind=kLoop, calls=%fused_computation.95 | loop fusion | flops 917504 | bytes 1048705 | tf_op jit(solution)/shard_map/convert_element_type | solution.py:23
  66.3 1.5 %collective-permute-start.2 = (bf16[16,64,128]{2,1,0:T(8,128)(2,1)}, bf16[16,64,128]{2,1,0:T(8,128)(2,1)S(1)}, u32[]{:S(2)}, u32[]{:S(2)}) collective-permute-start(bf16[16,64,128]{2,1,0:T(8,128)(2,1)} %fusion.41), channel_id=1, source_target_pairs={{0,8},{4,12},{8,0},{12,4},{16,24},{20,28},{24,16},{28,20},{1,9},{5... | collective-permute-start | bytes 786440 | tf_op jit(solution)/shard_map/ppermute | solution.py:23
  69.2 6.2 %collective-permute-done.3 = f32[16]{0:T(128)S(1)} collective-permute-done((f32[16]{0:T(128)S(1)}, f32[16]{0:T(128)S(1)}, u32[]{:S(2)}, u32[]{:S(2)}) %collective-permute-start.3) | collective-permute-done | bytes 96 | tf_op jit(solution)/shard_map/ppermute | solution.py:22
  75.4 2.0 %fusion.19 = bf16[16,64,128]{2,1,0:T(8,128)(2,1)} fusion(bf16[16,64,128]{2,1,0:T(8,128)(2,1)S(1)} %collective-permute-done.2, f32[16]{0:T(128)S(1)} %collective-permute-done.3, f32[16]{0:T(128)S(1)} %fusion.40, pred[]{:T(512)S(6)} %eq.14, f32[16,64,128]{2,1,0:T(8,128)S(1)} %fusion.20, f32[16]{0:T(128)} %collective-permute-done.1, ...), kind=kLoop, calls=%fused_computation.46 | loop fusion | flops 1703936 | bytes 1310978 | tf_op jit(solution)/shard_map/convert_element_type | solution.py:23
  77.3 1.5 %collective-permute-start.4 = (bf16[16,64,128]{2,1,0:T(8,128)(2,1)}, bf16[16,64,128]{2,1,0:T(8,128)(2,1)S(1)}, u32[]{:S(2)}, u32[]{:S(2)}) collective-permute-start(bf16[16,64,128]{2,1,0:T(8,128)(2,1)} %fusion.19), channel_id=1, source_target_pairs={{0,16},{4,20},{8,24},{12,28},{16,0},{20,4},{24,8},{28,12},{1,17},{... | collective-permute-start | bytes 786440 | tf_op jit(solution)/shard_map/ppermute | solution.py:23
  79.2 1.6 %copy.94 = f32[256,16]{0,1:T(8,128)} copy(f32[256,16]{1,0:T(8,128)} %get-tuple-element.63) | data formatting | bytes 32768 | tf_op jit(solution)/shard_map/transpose | solution.py:355
  80.9 1.5 %copy.88 = f32[16,256]{0,1:T(8,128)} copy(f32[16,256]{1,0:T(8,128)} %get-tuple-element.50) | data formatting | bytes 32768 | tf_op jit(solution)/shard_map/reduce_sum | solution.py:347
  82.4 1.5 %copy.87 = f32[16,256]{0,1:T(8,128)} copy(f32[16,256]{1,0:T(8,128)} %get-tuple-element.51) | data formatting | bytes 32768 | tf_op jit(solution)/shard_map/reduce_sum | solution.py:347
  84.4 0.9 collective-permute-done.4
  85.3 1.5 %convolution_bitcast_fusion.2 = f32[128,256]{1,0:T(8,128)S(1)} fusion(f32[256,16,64]{0,2,1:T(8,128)S(1)} %bitcast.104, f32[256,16]{0,1:T(8,128)S(1)} %copy.83, bf16[16,64,128]{2,1,0:T(8,128)(2,1)S(1)} %collective-permute-done.2, bf16[16,64,128]{2,1,0:T(8,128)(2,1)} %collective-permute-done, bf16[16,64,128]{2,1,0:T(8,128)(2,1)S(1)} %collective-permute-done.4, ...), kind=kOutput, calls=%fused_computation.20 | convolution fusion | flops 69074944 | bytes 1982595 | tf_op jit(solution)/shard_map/jhp,hpn->nj/dot_general | solution.py:344
  87.1 2.3 %multiply_reduce_fusion.1 = (f32[256,16]{0,1:T(8,128)S(1)}, f32[256,16]{0,1:T(8,128)S(1)}, bf16[256,16,64]{0,2,1:T(8,128)(2,1)S(1)}, f32[16]{0:T(128)S(1)}) fusion(f32[256,1024]{0,1:T(8,128)S(1)} %copy.84, f32[256,16,64]{0,2,1:T(8,128)} %fusion.8, f32[256,16]{0,1:T(8,128)} %copy.94, bf16[256,16,64]{0,2,1:T(8,128)(2,1)S(1)} %bitcast.99, f32[16]{0:T(128)} %param.22, ...), kind=kOutput, calls=%fused_computation.29 | convolution fusion | flops 72474608 | bytes 5128451 | tf_op jit(solution)/shard_map/jn,hpn->jhp/dot_general | solution.py:331
  89.5 1.1 fusion.35
  90.6 1.4 multiply_reduce_fusion.2
  93.7 0.7 copy.97
  94.4 1.0 copy.96.x_ref
  95.4 0.7 pad_maximum_fusion.bc_ref
  96.7 45.2 %matmul_scatter.1 = (bf16[1024,256]{1,0:T(8,128)(2,1)}, bf16[64,256]{1,0:T(8,128)(2,1)}, f32[8,128]{1,0:T(8,128)}) custom-call(bf16[4096,1024]{1,0:T(8,128)(2,1)} %w_hbm.3, bf16[256,1024]{1,0:T(8,128)(2,1)} %copy.96.x_ref, f32[256,256]{1,0:T(8,128)} %pad_maximum_fusion.bc_ref, f32[8,128]{1,0:T(8,128)} %select_maximum_fusion.p_ref), custom_call_target="tpu_custom_call" | custom-call | tf_op jit(solution)/shard_map/matmul_scatter/pallas_call | solution.py:261
  141.9 1.3 slice_multiply_fusion
  143.1 1.9 %copy.105 = bf16[1024,256]{1,0:T(8,128)(2,1)} copy(bf16[1024,256]{1,0:T(8,128)(2,1)} %get-tuple-element.72) | data formatting | bytes 1048576
  145.0 1.4 copy.106
  (85 shorter events, 9.5 us)
Async XLA Ops:
  0.6 51.9 %copy-start = (bf16[256,128]{1,0:T(8,128)(2,1)S(1)}, bf16[256,128]{1,0:T(8,128)(2,1)}, u32[]{:S(2)}) copy-start(bf16[256,128]{1,0:T(8,128)(2,1)} %param.17) | copy-start | bytes 196612
  1.3 1.6 %copy-start.18 = (f32[16]{0:T(128)}, f32[16]{0:T(128)S(1)}, u32[]{:S(2)}) copy-start(f32[16]{0:T(128)S(1)} %exponential_negate_fusion) | copy-start | bytes 196
  4.5 60.0 %collective-permute-start.1 = (f32[16]{0:T(128)}, f32[16]{0:T(128)}, u32[]{:S(2)}, u32[]{:S(2)}) collective-permute-start(f32[16]{0:T(128)} %fusion.39), channel_id=1, source_target_pairs={{0,4},{4,0},{8,12},{12,8},{16,20},{20,16},{24,28},{28,24},{1,5},{5... | collective-permute-start | bytes 200 | tf_op jit(solution)/shard_map/ppermute | solution.py:22
  5.0 44.9 %copy-start.17 = (f32[16]{0:T(128)}, f32[16]{0:T(128)S(1)}, u32[]{:S(2)}) copy-start(f32[16]{0:T(128)S(1)} %slice_bitcast_fusion) | copy-start | bytes 196
  5.0 44.9 %copy-start.13 = (f32[16]{0:T(128)S(1)}, f32[16]{0:T(128)}, u32[]{:S(2)}) copy-start(f32[16]{0:T(128)} %param.20) | copy-start | bytes 196
  5.0 45.8 %copy-start.5 = (bf16[256,128]{1,0:T(8,128)(2,1)S(1)}, bf16[256,128]{1,0:T(8,128)(2,1)}, u32[]{:S(2)}) copy-start(bf16[256,128]{1,0:T(8,128)(2,1)} %param.18) | copy-start | bytes 196612
  48.5 6.0 %copy-start.1 = (bf16[256,1024]{1,0:T(8,128)(2,1)S(1)}, bf16[256,1024]{1,0:T(8,128)(2,1)}, u32[]{:S(2)}) copy-start(bf16[256,1024]{1,0:T(8,128)(2,1)} %gather_matmul.1) | copy-start | bytes 1572868
  49.9 4.3 %copy-start.2 = (bf16[256,1024]{0,1:T(8,128)(2,1)}, bf16[256,1024]{0,1:T(8,128)(2,1)S(1)}, u32[]{:S(2)}) copy-start(bf16[256,1024]{0,1:T(8,128)(2,1)S(1)} %copy.76) | copy-start | bytes 1572868
  51.9 12.6 %collective-permute-start = (bf16[16,64,128]{2,1,0:T(8,128)(2,1)}, bf16[16,64,128]{2,1,0:T(8,128)(2,1)}, u32[]{:S(2)}, u32[]{:S(2)}) collective-permute-start(bf16[16,64,128]{2,1,0:T(8,128)(2,1)} %convert_element_type.69), channel_id=1, source_target_pairs={{0,4},{4,0},{8,12},{12,8},{16,20},{20,16},{24,28},{28,24},{1,5},{5... | collective-permute-start | bytes 786440 | tf_op jit(solution)/shard_map/ppermute | solution.py:23
  54.6 3.5 %copy-start.3 = (bf16[256,1024]{0,1:T(8,128)(2,1)S(1)}, bf16[256,1024]{0,1:T(8,128)(2,1)}, u32[]{:S(2)}) copy-start(bf16[256,1024]{0,1:T(8,128)(2,1)} %copy-done.2) | copy-start | bytes 1572868
  58.1 4.1 %copy-start.9 = (f32[256,256]{1,0:T(8,128)S(1)}, f32[256,256]{1,0:T(8,128)}, u32[]{:S(2)}) copy-start(f32[256,256]{1,0:T(8,128)} %fusion.45) | copy-start | bytes 786436
  58.1 4.1 %copy-start.10 = (pred[256,256]{1,0:T(8,128)(4,1)S(1)}, pred[256,256]{1,0:T(8,128)(4,1)}, u32[]{:S(2)}) copy-start(pred[256,256]{1,0:T(8,128)(4,1)} %iota_compare_fusion) | copy-start | bytes 196612
  62.2 5.7 %copy-start.6 = (f32[256,128]{0,1:T(8,128)S(1)}, f32[256,128]{0,1:T(8,128)}, u32[]{:S(2)}) copy-start(f32[256,128]{0,1:T(8,128)} %convolution_bitcast_fusion.1) | copy-start | bytes 393220
  62.2 16.7 %copy-start.4 = (bf16[1,1024,128]{2,1,0:T(8,128)(2,1)S(1)}, bf16[1,1024,128]{2,1,0:T(8,128)(2,1)}, u32[]{:S(2)}) copy-start(bf16[1,1024,128]{2,1,0:T(8,128)(2,1)} %param.23) | copy-start | bytes 786436
  62.2 18.6 %copy-start.7 = (f32[256,16]{1,0:T(8,128)S(1)}, f32[256,16]{1,0:T(8,128)}, u32[]{:S(2)}) copy-start(f32[256,16]{1,0:T(8,128)} %get-tuple-element.64) | copy-start | bytes 49156
  64.5 22.6 %copy-start.11 = (f32[256,16]{0,1:T(8,128)S(1)}, f32[256,16]{0,1:T(8,128)}, u32[]{:S(2)}) copy-start(f32[256,16]{0,1:T(8,128)} %copy.75) | copy-start | bytes 49156
  66.3 9.0 %collective-permute-start.2 = (bf16[16,64,128]{2,1,0:T(8,128)(2,1)}, bf16[16,64,128]{2,1,0:T(8,128)(2,1)S(1)}, u32[]{:S(2)}, u32[]{:S(2)}) collective-permute-start(bf16[16,64,128]{2,1,0:T(8,128)(2,1)} %fusion.41), channel_id=1, source_target_pairs={{0,8},{4,12},{8,0},{12,4},{16,24},{20,28},{24,16},{28,20},{1,9},{5... | collective-permute-start | bytes 786440 | tf_op jit(solution)/shard_map/ppermute | solution.py:23
  68.7 6.7 %collective-permute-start.3 = (f32[16]{0:T(128)S(1)}, f32[16]{0:T(128)S(1)}, u32[]{:S(2)}, u32[]{:S(2)}) collective-permute-start(f32[16]{0:T(128)S(1)} %fusion.40), channel_id=1, source_target_pairs={{0,8},{4,12},{8,0},{12,4},{16,24},{20,28},{24,16},{28,20},{1,9},{5... | collective-permute-start | bytes 200 | tf_op jit(solution)/shard_map/ppermute | solution.py:22
  77.3 8.0 %collective-permute-start.4 = (bf16[16,64,128]{2,1,0:T(8,128)(2,1)}, bf16[16,64,128]{2,1,0:T(8,128)(2,1)S(1)}, u32[]{:S(2)}, u32[]{:S(2)}) collective-permute-start(bf16[16,64,128]{2,1,0:T(8,128)(2,1)} %fusion.19), channel_id=1, source_target_pairs={{0,16},{4,20},{8,24},{12,28},{16,0},{20,4},{24,8},{28,12},{1,17},{... | collective-permute-start | bytes 786440 | tf_op jit(solution)/shard_map/ppermute | solution.py:23
  80.8 4.5 %copy-start.12 = (f32[256,16]{0,1:T(8,128)}, f32[256,16]{0,1:T(8,128)S(1)}, u32[]{:S(2)}) copy-start(f32[256,16]{0,1:T(8,128)S(1)} %copy.83) | copy-start | bytes 49156
  84.4 4.9 %copy-start.15 = (f32[16]{0:T(128)}, f32[16]{0:T(128)S(1)}, u32[]{:S(2)}) copy-start(f32[16]{0:T(128)S(1)} %get-tuple-element.57) | copy-start | bytes 196
  84.4 4.9 %copy-start.16 = (f32[16]{0:T(128)}, f32[16]{0:T(128)S(1)}, u32[]{:S(2)}) copy-start(f32[16]{0:T(128)S(1)} %get-tuple-element.58) | copy-start | bytes 196
  85.3 1.5 %copy-start.8 = (bf16[16,64,128]{2,1,0:T(8,128)(2,1)}, bf16[16,64,128]{2,1,0:T(8,128)(2,1)S(1)}, u32[]{:S(2)}) copy-start(bf16[16,64,128]{2,1,0:T(8,128)(2,1)S(1)} %collective-permute-done.4) | copy-start | bytes 786436
  87.0 6.5 %copy-start.14 = (f32[16]{0:T(128)S(1)}, f32[16]{0:T(128)}, u32[]{:S(2)}) copy-start(f32[16]{0:T(128)} %param.20) | copy-start | bytes 196
  87.1 6.5 %copy-start.19 = (f32[16]{0:T(128)S(1)}, f32[16]{0:T(128)}, u32[]{:S(2)}) copy-start(f32[16]{0:T(128)} %copy-done.18) | copy-start | bytes 196

commit v4 on v3

--- a/solution.py
+++ b/solution.py
@@ -12,7 +12,7 @@
     return [(place, place ^ distance) for place in range(count)]
 
 
-def entering(decay, state, axis):
+def entering(decay, state, axis, beside):
     count, mine = (lax.axis_size(axis), lax.axis_index(axis))
     carried = jnp.zeros_like(state)
     reach = jnp.ones_like(decay)
@@ -20,7 +20,10 @@
     while distance < count:
         pairs = partners(count, distance)
         other_decay = lax.ppermute(decay, axis, pairs)
-        other_state = lax.ppermute(state.astype(jnp.bfloat16), axis, pairs).astype(jnp.float32)
+        other_state = lax.ppermute(state.astype(jnp.bfloat16), axis, pairs)
+        if distance == 1:
+            other_state, beside = lax.optimization_barrier((other_state, beside))
+        other_state = other_state.astype(jnp.float32)
         earlier = (mine // distance) % 2 == 0
         carried = jnp.where(earlier, carried + reach[:, None, None] * other_state, carried)
         reach = jnp.where(earlier, reach * other_decay, reach)
@@ -31,7 +34,7 @@
         )
         decay = decay * other_decay
         distance *= 2
-    return carried
+    return carried, beside
 
 
 LAST = (((1,), (1,)), ((), ()))
@@ -132,7 +135,7 @@
     return pl.pallas_call(
         functools.partial(gather_matmul_kernel, n),
         out_shape=jax.ShapeDtypeStruct((tokens, width), jnp.bfloat16),
-        in_specs=[vmem, pl.BlockSpec(memory_space=pl.ANY)],
+        in_specs=[vmem, pl.BlockSpec(memory_space=pltpu.HBM)],
         out_specs=vmem,
         scratch_shapes=[
             pltpu.VMEM((n - 1, tokens, depth), jnp.bfloat16),
@@ -143,7 +146,7 @@
             pltpu.SemaphoreType.DMA((n,)),
         ],
         compiler_params=pltpu.CompilerParams(
-            collective_id=0, has_side_effects=True, vmem_limit_bytes=60 * 2**20
+            collective_id=0, has_side_effects=True, vmem_limit_bytes=52 * 2**20
         ),
         name="gather_matmul",
     )(x, w)
@@ -265,7 +268,7 @@
             jax.ShapeDtypeStruct((bc_here, tokens), jnp.bfloat16),
             jax.ShapeDtypeStruct((8, 128), jnp.float32),
         ),
-        in_specs=[pl.BlockSpec(memory_space=pl.ANY), vmem, vmem, vmem],
+        in_specs=[pl.BlockSpec(memory_space=pltpu.HBM), vmem, vmem, vmem],
         out_specs=(vmem, vmem, vmem),
         scratch_shapes=[
             pltpu.VMEM(w.shape, jnp.bfloat16),
@@ -279,7 +282,7 @@
             pltpu.SemaphoreType.DMA((s - 1,)),
         ],
         compiler_params=pltpu.CompilerParams(
-            collective_id=1, has_side_effects=True, vmem_limit_bytes=60 * 2**20
+            collective_id=1, has_side_effects=True, vmem_limit_bytes=52 * 2**20
         ),
         name="matmul_scatter",
     )(w, x, bc, padded)
@@ -307,7 +310,8 @@
     start_decay = jnp.exp(cumlog)
     dy_decay = (dy_heads.astype(jnp.float32) * start_decay.T[:, :, None]).astype(jnp.bfloat16)
     local_state = jnp.einsum("ihp,in->hpn", dy_decay, c_in, preferred_element_type=jnp.float32)
-    dy_heads, local_state = lax.optimization_barrier((dy_heads, local_state))
+    end_total = jnp.exp(cumlog[:, -1])
+    carried, dy_heads = entering(end_total, local_state, "seq", dy_heads)
     dy_wide = dy_heads.astype(jnp.float32)
     scores = lax.dot_general(c_in, b_in, contract_last, preferred_element_type=jnp.float32)
     step_rows = step_size.T
@@ -316,7 +320,6 @@
     kernel = (scores[None] * decay_mask).astype(jnp.bfloat16)
     intra_back = jnp.einsum("hij,ihp->jhp", kernel, dy_heads, preferred_element_type=jnp.float32)
     masked_dots = (pair_dots * decay_mask).astype(jnp.bfloat16)
-    end_total = jnp.exp(cumlog[:, -1])
     entry_state = states.reshape(group_heads, head_dim, state_dim)
     db_intra = jnp.einsum("hij,in->nj", masked_dots, c_in, preferred_element_type=jnp.float32)
     dc_intra = jnp.einsum("hij,jn->ni", masked_dots, b_in, preferred_element_type=jnp.float32)
@@ -326,7 +329,6 @@
     state_terms = start_decay * jnp.sum(dy_wide * ystate, axis=2).T
     skip_terms = jnp.sum(dy_wide * x_wide, axis=(0, 2))
 
-    carried = entering(end_total, local_state, "seq")
     carried_bf = carried.astype(jnp.bfloat16)
     state_back = jnp.einsum("jn,hpn->jhp", b_in, carried_bf, preferred_element_type=jnp.float32)
     end_decay = jnp.exp(cumlog[:, -1:] - cumlog)

time: 147 us -> 134 us (0.912)
  Pallas kernels: 88.7 us -> 84.1 us
  waiting for transfers between devices: 7.03 us -> 2.6 us
  local copies, waits for them, and re-layouts: 16.1 us -> 13.4 us
  other arithmetic: 15.5 us -> 12.8 us
    ppermute x2, waiting for transfers between devices: 6.16 us -> 0.84 us  [entering(): other_decay = lax.ppermute(decay, axis, pairs)]
    pallas_call x1, Pallas kernels: 45.2 us -> 42.4 us  [matmul_scatter(): pl.pallas_call(functools.partial(matmul_scatter_kernel, n, s), out_shape=...]
    pallas_call x1, Pallas kernels: 43.6 us -> 41.7 us  [gather_matmul(): pl.pallas_call(functools.partial(gather_matmul_kernel, n), out_shape=jax....]
    convert_element_type x3 -> x2, other arithmetic: 4.58 us -> 3.11 us  [entering(): other_state = lax.ppermute(state.astype(jnp.bfloat16), axis, pairs)]
  transfers between devices with their start and end apart: 5 -> 5, of which waited for: 2 -> 2; matrix products, arithmetic and copies ran while one was open for 15% -> 16% of each run, Pallas kernels for 30% -> 31%
where the time goes in v4:
time: 134 us; the launch traced here: 133 us
  Pallas kernels  84.1 us (63%)
  matrix products  14 us (10%)
  local copies, waits for them, and re-layouts  13.4 us (10%)
  other arithmetic  12.8 us (10%)
  starting transfers between devices  5.05 us (4%)
  waiting for transfers between devices  2.6 us (2%)
    pallas_call x1, Pallas kernels, matmul_scatter(): pl.pallas_call(functools.partial(matmul_scatter_kernel, n, s), out_shape=...  42.4 us
    pallas_call x1, Pallas kernels, gather_matmul(): pl.pallas_call(functools.partial(gather_matmul_kernel, n), out_shape=jax....  41.7 us
    dot_general x1, matrix products, shards(): jnp.einsum('ihp,jhp->hij', dy_heads, x_scaled, preferred_element_type=jnp...  4.06 us
    unnamed x44, local copies, waits for them, and re-layouts  4.03 us
    convert_element_type x2, other arithmetic, entering(): other_state = lax.ppermute(state.astype(jnp.bfloat16), axis, pairs)  3.11 us
    ppermute x3, starting transfers between devices, entering(): other_state = lax.ppermute(state.astype(jnp.bfloat16), axis, pairs)  3.07 us
  transfers between devices with their start and end apart: 5, of which 2 were waited for; matrix products, arithmetic and copies ran while one was open for 16% of the time, Pallas kernels for 31%

profile of v4, /device:TPU:0, one launch (start us, length us, event | category | flops | bytes accessed | tf_op | source)
XLA Modules:
  0.0 133.0 jit_solution(10653794114269920346)
XLA Ops:
  0.6 0.7 exponential_negate_fusion
  1.3 0.8 copy.74
  2.2 0.7 broadcast_multiply_fusion
  5.0 1.0 copy-done.1
  6.0 41.7 %gather_matmul.1 = bf16[256,1024]{1,0:T(8,128)(2,1)S(1)} custom-call(bf16[256,1024]{1,0:T(8,128)(2,1)S(1)} %copy-done.1, bf16[1024,4096]{1,0:T(8,128)(2,1)} %w_hbm.2), custom_call_target="tpu_custom_call" | custom-call | tf_op jit(solution)/shard_map/gather_matmul/pallas_call | solution.py:135
  48.0 0.8 fusion.30
  48.8 1.0 fusion.45
  50.5 0.9 fusion.46
  51.4 0.7 copy.94
  53.5 1.2 convolution_bitcast_fusion.1
  54.8 1.0 copy.75
  55.7 0.7 fusion.40
  56.4 1.5 %collective-permute-start.3 = (f32[16]{0:T(128)S(1)}, f32[16]{0:T(128)S(1)}, u32[]{:S(2)}, u32[]{:S(2)}) collective-permute-start(f32[16]{0:T(128)S(1)} %fusion.40), channel_id=1, source_target_pairs={{0,8},{4,12},{8,0},{12,4},{16,24},{20,28},{24,16},{28,20},{1,9},{5... | collective-permute-start | bytes 200 | tf_op jit(solution)/shard_map/ppermute | solution.py:22
  57.9 1.2 copy.84
  59.2 0.8 collective-permute-done.3
  60.0 1.3 broadcast_select_fusion
  61.3 1.1 fusion.41
  62.4 1.6 %collective-permute-start.2 = (bf16[16,64,128]{2,1,0:T(8,128)(2,1)S(1)}, bf16[16,64,128]{2,1,0:T(8,128)(2,1)S(1)}, u32[]{:S(2)}, u32[]{:S(2)}) collective-permute-start(bf16[16,64,128]{2,1,0:T(8,128)(2,1)S(1)} %fusion.41), channel_id=1, source_target_pairs={{0,8},{4,12},{8,0},{12,4},{16,24},{20,28},{24,16},{28,20},{1,9},{5... | collective-permute-start | bytes 786440 | tf_op jit(solution)/shard_map/ppermute | solution.py:23
  64.0 4.1 %fusion = (f32[16,256]{1,0:T(8,128)}, f32[16,256]{1,0:T(8,128)}, bf16[256,256]{1,0:T(8,128)(2,1)S(1)}) fusion(f32[16,256]{1,0:T(8,128)S(1)} %copy_bitcast_fusion, f32[256,256]{1,0:T(8,128)} %fusion.46, pred[256,256]{1,0:T(8,128)(4,1)} %iota_compare_fusion, bf16[256,16,64]{0,2,1:T(8,128)(2,1)S(1)} %bitcast.98, f32[256,16,64]{0,2,1:T(8,128)S(1)} %bitcast.105, ...), kind=kOutput, calls=%fused_computation.5 | convolution fusion | flops 146202624 | bytes 2097152 | tf_op jit(solution)/shard_map/ihp,jhp->hij/dot_general | solution.py:319
  68.1 2.3 %fusion.8 = f32[256,16,64]{0,2,1:T(8,128)} fusion(bf16[256,16,64]{0,2,1:T(8,128)(2,1)S(1)} %bitcast.99, f32[16,256]{1,0:T(8,128)S(1)} %copy_bitcast_fusion, f32[256,256]{1,0:T(8,128)S(1)} %copy-done.7, pred[256,256]{1,0:T(8,128)(4,1)S(1)} %copy-done.8), kind=kOutput, calls=%fused_computation.16 | convolution fusion | flops 139460608 | bytes 1916928 | tf_op jit(solution)/shard_map/hij,ihp->jhp/dot_general | solution.py:321
  70.4 2.0 %fusion.19 = bf16[16,64,128]{2,1,0:T(8,128)(2,1)} fusion(bf16[16,64,128]{2,1,0:T(8,128)(2,1)S(1)} %collective-permute-done.2, f32[16]{0:T(128)S(1)} %copy-done.15, f32[16]{0:T(128)S(1)} %copy-done.19, pred[]{:T(512)S(6)} %eq.14, f32[16,64,128]{2,1,0:T(8,128)S(1)} %get-tuple-element.69, f32[16]{0:T(128)} %collective-permute-done.1, ...), kind=kLoop, calls=%fused_computation.46 | loop fusion | flops 1703936 | bytes 1310978 | tf_op jit(solution)/shard_map/convert_element_type | solution.py:23
  72.4 1.5 %collective-permute-start.4 = (bf16[16,64,128]{2,1,0:T(8,128)(2,1)}, bf16[16,64,128]{2,1,0:T(8,128)(2,1)S(1)}, u32[]{:S(2)}, u32[]{:S(2)}) collective-permute-start(bf16[16,64,128]{2,1,0:T(8,128)(2,1)} %fusion.19), channel_id=1, source_target_pairs={{0,16},{4,20},{8,24},{12,28},{16,0},{20,4},{24,8},{28,12},{1,17},{... | collective-permute-start | bytes 786440 | tf_op jit(solution)/shard_map/ppermute | solution.py:23
  74.3 1.5 %copy.88 = f32[16,256]{0,1:T(8,128)} copy(f32[16,256]{1,0:T(8,128)} %get-tuple-element.50) | data formatting | bytes 32768 | tf_op jit(solution)/shard_map/reduce_sum | solution.py:349
  75.8 1.5 %copy.87 = f32[16,256]{0,1:T(8,128)} copy(f32[16,256]{1,0:T(8,128)} %get-tuple-element.51) | data formatting | bytes 32768 | tf_op jit(solution)/shard_map/reduce_sum | solution.py:349
  77.4 1.8 %collective-permute-done.4 = bf16[16,64,128]{2,1,0:T(8,128)(2,1)S(1)} collective-permute-done((bf16[16,64,128]{2,1,0:T(8,128)(2,1)}, bf16[16,64,128]{2,1,0:T(8,128)(2,1)S(1)}, u32[]{:S(2)}, u32[]{:S(2)}) %collective-permute-start.4) | collective-permute-done | bytes 262176 | tf_op jit(solution)/shard_map/ppermute | solution.py:23
  79.2 1.5 %convolution_bitcast_fusion.2 = f32[128,256]{1,0:T(8,128)S(1)} fusion(f32[256,16,64]{0,2,1:T(8,128)S(1)} %bitcast.106, f32[256,16]{0,1:T(8,128)} %copy.83, bf16[16,64,128]{2,1,0:T(8,128)(2,1)S(1)} %collective-permute-done.2, bf16[16,64,128]{2,1,0:T(8,128)(2,1)} %collective-permute-done, bf16[16,64,128]{2,1,0:T(8,128)(2,1)S(1)} %collective-permute-done.4, ...), kind=kOutput, calls=%fused_computation.20 | convolution fusion | flops 69074944 | bytes 1982595 | tf_op jit(solution)/shard_map/jhp,hpn->nj/dot_general | solution.py:346
  81.0 2.3 %multiply_reduce_fusion.1 = (f32[256,16]{0,1:T(8,128)S(1)}, f32[256,16]{0,1:T(8,128)S(1)}, bf16[256,16,64]{0,2,1:T(8,128)(2,1)S(1)}, f32[16]{0:T(128)S(1)}) fusion(f32[256,1024]{0,1:T(8,128)S(1)} %copy.84, f32[256,16,64]{0,2,1:T(8,128)} %fusion.8, f32[256,16]{0,1:T(8,128)S(1)} %copy-done.9, bf16[256,16,64]{0,2,1:T(8,128)(2,1)S(1)} %bitcast.101, ...), kind=kOutput, calls=%fused_computation.29 | convolution fusion | flops 72474608 | bytes 5128451 | tf_op jit(solution)/shard_map/jn,hpn->jhp/dot_general | solution.py:333
  83.4 1.1 fusion.35
  84.5 1.4 %multiply_reduce_fusion.2 = f32[16]{0:T(128)S(1)} fusion(bf16[16,64,128]{2,1,0:T(8,128)(2,1)S(1)} %bitcast.104, bf16[16,64,128]{2,1,0:T(8,128)(2,1)} %copy-done.6, f32[16]{0:T(128)} %get-tuple-element.57, bf16[16,64,128]{2,1,0:T(8,128)(2,1)S(1)} %collective-permute-done.2, f32[16]{0:T(128)} %get-tuple-element.58, ...), kind=kLoop, calls=%fused_computation.49 | loop fusion | flops 1703920 | bytes 1048771 | tf_op jit(solution)/shard_map/reduce_sum | solution.py:350
  87.6 0.7 copy.97
  88.6 42.4 %matmul_scatter.1 = (bf16[1024,256]{1,0:T(8,128)(2,1)S(1)}, bf16[64,256]{1,0:T(8,128)(2,1)S(1)}, f32[8,128]{1,0:T(8,128)S(1)}) custom-call(bf16[4096,1024]{1,0:T(8,128)(2,1)} %w_hbm.3, bf16[256,1024]{1,0:T(8,128)(2,1)S(1)} %copy.96.x_ref, f32[256,256]{1,0:T(8,128)S(1)} %pad_maximum_fusion.bc_ref, f32[8,128]{1,0:T(8,128)S(1)} %select_maximum_fusion.p_ref), custom_call_target="tpu_custom_call" | custom-call | tf_op jit(solution)/shard_map/matmul_scatter/pallas_call | solution.py:264
  131.6 0.8 copy.105
  (84 shorter events, 8.5 us)
Async XLA Ops:
  0.6 49.9 %copy-start = (bf16[256,128]{1,0:T(8,128)(2,1)S(1)}, bf16[256,128]{1,0:T(8,128)(2,1)}, u32[]{:S(2)}) copy-start(bf16[256,128]{1,0:T(8,128)(2,1)} %param.17) | copy-start | bytes 196612
  1.3 1.6 %copy-start.16 = (f32[16]{0:T(128)}, f32[16]{0:T(128)S(1)}, u32[]{:S(2)}) copy-start(f32[16]{0:T(128)S(1)} %exponential_negate_fusion) | copy-start | bytes 196
  4.5 51.3 %collective-permute-start.1 = (f32[16]{0:T(128)}, f32[16]{0:T(128)}, u32[]{:S(2)}, u32[]{:S(2)}) collective-permute-start(f32[16]{0:T(128)} %fusion.39), channel_id=1, source_target_pairs={{0,4},{4,0},{8,12},{12,8},{16,20},{20,16},{24,28},{28,24},{1,5},{5... | collective-permute-start | bytes 200 | tf_op jit(solution)/shard_map/ppermute | solution.py:22
  5.0 1.0 copy-start.1
  6.0 41.9 %copy-start.13 = (f32[16]{0:T(128)}, f32[16]{0:T(128)S(1)}, u32[]{:S(2)}) copy-start(f32[16]{0:T(128)S(1)} %slice_bitcast_fusion) | copy-start | bytes 196
  6.0 41.9 %copy-start.11 = (f32[16]{0:T(128)S(1)}, f32[16]{0:T(128)}, u32[]{:S(2)}) copy-start(f32[16]{0:T(128)} %param.20) | copy-start | bytes 196
  6.0 42.8 %copy-start.5 = (bf16[256,128]{1,0:T(8,128)(2,1)S(1)}, bf16[256,128]{1,0:T(8,128)(2,1)}, u32[]{:S(2)}) copy-start(bf16[256,128]{1,0:T(8,128)(2,1)} %param.18) | copy-start | bytes 196612
  47.9 4.9 %copy-start.2 = (bf16[256,1024]{0,1:T(8,128)(2,1)}, bf16[256,1024]{0,1:T(8,128)(2,1)S(1)}, u32[]{:S(2)}) copy-start(bf16[256,1024]{0,1:T(8,128)(2,1)S(1)} %copy.76) | copy-start | bytes 1572868
  49.8 11.4 %collective-permute-start = (bf16[16,64,128]{2,1,0:T(8,128)(2,1)}, bf16[16,64,128]{2,1,0:T(8,128)(2,1)}, u32[]{:S(2)}, u32[]{:S(2)}) collective-permute-start(bf16[16,64,128]{2,1,0:T(8,128)(2,1)} %get-tuple-element.68), channel_id=1, source_target_pairs={{0,4},{4,0},{8,12},{12,8},{16,20},{20,16},{24,28},{28,24},{1,5},{5... | collective-permute-start | bytes 786440 | tf_op jit(solution)/shard_map/ppermute | solution.py:23
  53.2 10.8 %copy-start.3 = (bf16[256,1024]{0,1:T(8,128)(2,1)S(1)}, bf16[256,1024]{0,1:T(8,128)(2,1)}, u32[]{:S(2)}) copy-start(bf16[256,1024]{0,1:T(8,128)(2,1)} %copy-done.2) | copy-start | bytes 1572868
  55.7 8.3 %copy-start.10 = (f32[256,16]{0,1:T(8,128)}, f32[256,16]{0,1:T(8,128)S(1)}, u32[]{:S(2)}) copy-start(f32[256,16]{0,1:T(8,128)S(1)} %copy.75) | copy-start | bytes 49156
  56.4 7.6 %copy-start.18 = (f32[16]{0:T(128)}, f32[16]{0:T(128)S(1)}, u32[]{:S(2)}) copy-start(f32[16]{0:T(128)S(1)} %fusion.40) | copy-start | bytes 196
  56.4 3.6 %collective-permute-start.3 = (f32[16]{0:T(128)S(1)}, f32[16]{0:T(128)S(1)}, u32[]{:S(2)}, u32[]{:S(2)}) collective-permute-start(f32[16]{0:T(128)S(1)} %fusion.40), channel_id=1, source_target_pairs={{0,8},{4,12},{8,0},{12,4},{16,24},{20,28},{24,16},{28,20},{1,9},{5... | collective-permute-start | bytes 200 | tf_op jit(solution)/shard_map/ppermute | solution.py:22
  60.0 4.0 %copy-start.14 = (f32[16]{0:T(128)}, f32[16]{0:T(128)S(1)}, u32[]{:S(2)}) copy-start(f32[16]{0:T(128)S(1)} %collective-permute-done.3) | copy-start | bytes 196
  62.4 8.0 %collective-permute-start.2 = (bf16[16,64,128]{2,1,0:T(8,128)(2,1)S(1)}, bf16[16,64,128]{2,1,0:T(8,128)(2,1)S(1)}, u32[]{:S(2)}, u32[]{:S(2)}) collective-permute-start(bf16[16,64,128]{2,1,0:T(8,128)(2,1)S(1)} %fusion.41), channel_id=1, source_target_pairs={{0,8},{4,12},{8,0},{12,4},{16,24},{20,28},{24,16},{28,20},{1,9},{5... | collective-permute-start | bytes 786440 | tf_op jit(solution)/shard_map/ppermute | solution.py:23
  64.0 4.1 %copy-start.7 = (f32[256,256]{1,0:T(8,128)S(1)}, f32[256,256]{1,0:T(8,128)}, u32[]{:S(2)}) copy-start(f32[256,256]{1,0:T(8,128)} %fusion.46) | copy-start | bytes 786436
  64.0 4.1 %copy-start.8 = (pred[256,256]{1,0:T(8,128)(4,1)S(1)}, pred[256,256]{1,0:T(8,128)(4,1)}, u32[]{:S(2)}) copy-start(pred[256,256]{1,0:T(8,128)(4,1)} %iota_compare_fusion) | copy-start | bytes 196612
  68.1 2.3 %copy-start.15 = (f32[16]{0:T(128)S(1)}, f32[16]{0:T(128)}, u32[]{:S(2)}) copy-start(f32[16]{0:T(128)} %copy-done.14) | copy-start | bytes 196
  68.1 2.3 %copy-start.19 = (f32[16]{0:T(128)S(1)}, f32[16]{0:T(128)}, u32[]{:S(2)}) copy-start(f32[16]{0:T(128)} %copy-done.18) | copy-start | bytes 196
  68.1 5.8 %copy-start.4 = (bf16[1,1024,128]{2,1,0:T(8,128)(2,1)S(1)}, bf16[1,1024,128]{2,1,0:T(8,128)(2,1)}, u32[]{:S(2)}) copy-start(bf16[1,1024,128]{2,1,0:T(8,128)(2,1)} %param.23) | copy-start | bytes 786436
  70.4 10.6 %copy-start.9 = (f32[256,16]{0,1:T(8,128)S(1)}, f32[256,16]{0,1:T(8,128)}, u32[]{:S(2)}) copy-start(f32[256,16]{0,1:T(8,128)} %copy.94) | copy-start | bytes 49156
  72.4 6.8 %collective-permute-start.4 = (bf16[16,64,128]{2,1,0:T(8,128)(2,1)}, bf16[16,64,128]{2,1,0:T(8,128)(2,1)S(1)}, u32[]{:S(2)}, u32[]{:S(2)}) collective-permute-start(bf16[16,64,128]{2,1,0:T(8,128)(2,1)} %fusion.19), channel_id=1, source_target_pairs={{0,16},{4,20},{8,24},{12,28},{16,0},{20,4},{24,8},{28,12},{1,17},{... | collective-permute-start | bytes 786440 | tf_op jit(solution)/shard_map/ppermute | solution.py:23
  79.2 1.5 %copy-start.6 = (bf16[16,64,128]{2,1,0:T(8,128)(2,1)}, bf16[16,64,128]{2,1,0:T(8,128)(2,1)S(1)}, u32[]{:S(2)}) copy-start(bf16[16,64,128]{2,1,0:T(8,128)(2,1)S(1)} %collective-permute-done.4) | copy-start | bytes 786436
  81.0 6.5 %copy-start.12 = (f32[16]{0:T(128)S(1)}, f32[16]{0:T(128)}, u32[]{:S(2)}) copy-start(f32[16]{0:T(128)} %param.20) | copy-start | bytes 196
  81.0 6.5 %copy-start.17 = (f32[16]{0:T(128)S(1)}, f32[16]{0:T(128)}, u32[]{:S(2)}) copy-start(f32[16]{0:T(128)} %copy-done.16) | copy-start | bytes 196

commit v5 on v4

--- a/solution.py
+++ b/solution.py
@@ -39,7 +39,7 @@
 
 LAST = (((1,), (1,)), ((), ()))
 MESH = pl.DeviceIdType.MESH
-CHUNKS = 2
+CHUNKS = 4
 
 
 def tile_of(extent):

time: 134 us -> 135 us (level)
  no operation moved by 1% of the time
where the time goes in v5:
time: 135 us; the launch traced here: 134 us
  Pallas kernels  85.4 us (63%)
  matrix products  14 us (10%)
  local copies, waits for them, and re-layouts  13.4 us (10%)
  other arithmetic  12.8 us (9%)
  starting transfers between devices  5.07 us (4%)
  waiting for transfers between devices  2.58 us (2%)
    pallas_call x1, Pallas kernels, matmul_scatter(): pl.pallas_call(functools.partial(matmul_scatter_kernel, n, s), out_shape=...  43.5 us
    pallas_call x1, Pallas kernels, gather_matmul(): pl.pallas_call(functools.partial(gather_matmul_kernel, n), out_shape=jax....  41.9 us
    dot_general x1, matrix products, shards(): jnp.einsum('ihp,jhp->hij', dy_heads, x_scaled, preferred_element_type=jnp...  4.07 us
    unnamed x44, local copies, waits for them, and re-layouts  4.03 us
    convert_element_type x2, other arithmetic, entering(): other_state = lax.ppermute(state.astype(jnp.bfloat16), axis, pairs)  3.11 us
    ppermute x3, starting transfers between devices, entering(): other_state = lax.ppermute(state.astype(jnp.bfloat16), axis, pairs)  3.08 us
  transfers between devices with their start and end apart: 5, of which 2 were waited for; matrix products, arithmetic and copies ran while one was open for 16% of the time, Pallas kernels for 31%

profile of v5, /device:TPU:0, one launch (start us, length us, event | category | flops | bytes accessed | tf_op | source)
XLA Modules:
  0.0 134.3 jit_solution(4538111146932794397)
XLA Ops:
  0.6 0.7 exponential_negate_fusion
  1.3 0.8 copy.74
  2.2 0.7 broadcast_multiply_fusion
  5.0 1.0 copy-done.1
  6.0 41.9 %gather_matmul.1 = bf16[256,1024]{1,0:T(8,128)(2,1)S(1)} custom-call(bf16[256,1024]{1,0:T(8,128)(2,1)S(1)} %copy-done.1, bf16[1024,4096]{1,0:T(8,128)(2,1)} %w_hbm.2), custom_call_target="tpu_custom_call" | custom-call | tf_op jit(solution)/shard_map/gather_matmul/pallas_call | solution.py:135
  48.2 0.8 fusion.30
  49.1 1.0 fusion.45
  50.7 0.9 fusion.46
  51.6 0.7 copy.94
  53.8 1.2 convolution_bitcast_fusion.1
  55.0 1.0 copy.75
  56.0 0.7 fusion.40
  56.7 1.5 %collective-permute-start.3 = (f32[16]{0:T(128)S(1)}, f32[16]{0:T(128)S(1)}, u32[]{:S(2)}, u32[]{:S(2)}) collective-permute-start(f32[16]{0:T(128)S(1)} %fusion.40), channel_id=1, source_target_pairs={{0,8},{4,12},{8,0},{12,4},{16,24},{20,28},{24,16},{28,20},{1,9},{5... | collective-permute-start | bytes 200 | tf_op jit(solution)/shard_map/ppermute | solution.py:22
  58.1 1.2 copy.84
  59.4 0.8 collective-permute-done.3
  60.2 1.3 broadcast_select_fusion
  61.5 1.1 fusion.41
  62.7 1.6 %collective-permute-start.2 = (bf16[16,64,128]{2,1,0:T(8,128)(2,1)S(1)}, bf16[16,64,128]{2,1,0:T(8,128)(2,1)S(1)}, u32[]{:S(2)}, u32[]{:S(2)}) collective-permute-start(bf16[16,64,128]{2,1,0:T(8,128)(2,1)S(1)} %fusion.41), channel_id=1, source_target_pairs={{0,8},{4,12},{8,0},{12,4},{16,24},{20,28},{24,16},{28,20},{1,9},{5... | collective-permute-start | bytes 786440 | tf_op jit(solution)/shard_map/ppermute | solution.py:23
  64.2 4.1 %fusion = (f32[16,256]{1,0:T(8,128)}, f32[16,256]{1,0:T(8,128)}, bf16[256,256]{1,0:T(8,128)(2,1)S(1)}) fusion(f32[16,256]{1,0:T(8,128)S(1)} %copy_bitcast_fusion, f32[256,256]{1,0:T(8,128)} %fusion.46, pred[256,256]{1,0:T(8,128)(4,1)} %iota_compare_fusion, bf16[256,16,64]{0,2,1:T(8,128)(2,1)S(1)} %bitcast.98, f32[256,16,64]{0,2,1:T(8,128)S(1)} %bitcast.105, ...), kind=kOutput, calls=%fused_computation.5 | convolution fusion | flops 146202624 | bytes 2097152 | tf_op jit(solution)/shard_map/ihp,jhp->hij/dot_general | solution.py:319
  68.3 2.3 %fusion.8 = f32[256,16,64]{0,2,1:T(8,128)} fusion(bf16[256,16,64]{0,2,1:T(8,128)(2,1)S(1)} %bitcast.99, f32[16,256]{1,0:T(8,128)S(1)} %copy_bitcast_fusion, f32[256,256]{1,0:T(8,128)S(1)} %copy-done.7, pred[256,256]{1,0:T(8,128)(4,1)S(1)} %copy-done.8), kind=kOutput, calls=%fused_computation.16 | convolution fusion | flops 139460608 | bytes 1916928 | tf_op jit(solution)/shard_map/hij,ihp->jhp/dot_general | solution.py:321
  70.6 2.0 %fusion.19 = bf16[16,64,128]{2,1,0:T(8,128)(2,1)} fusion(bf16[16,64,128]{2,1,0:T(8,128)(2,1)S(1)} %collective-permute-done.2, f32[16]{0:T(128)S(1)} %copy-done.15, f32[16]{0:T(128)S(1)} %copy-done.19, pred[]{:T(512)S(6)} %eq.14, f32[16,64,128]{2,1,0:T(8,128)S(1)} %get-tuple-element.69, f32[16]{0:T(128)} %collective-permute-done.1, ...), kind=kLoop, calls=%fused_computation.46 | loop fusion | flops 1703936 | bytes 1310978 | tf_op jit(solution)/shard_map/convert_element_type | solution.py:23
  72.6 1.5 %collective-permute-start.4 = (bf16[16,64,128]{2,1,0:T(8,128)(2,1)}, bf16[16,64,128]{2,1,0:T(8,128)(2,1)S(1)}, u32[]{:S(2)}, u32[]{:S(2)}) collective-permute-start(bf16[16,64,128]{2,1,0:T(8,128)(2,1)} %fusion.19), channel_id=1, source_target_pairs={{0,16},{4,20},{8,24},{12,28},{16,0},{20,4},{24,8},{28,12},{1,17},{... | collective-permute-start | bytes 786440 | tf_op jit(solution)/shard_map/ppermute | solution.py:23
  74.5 1.5 %copy.88 = f32[16,256]{0,1:T(8,128)} copy(f32[16,256]{1,0:T(8,128)} %get-tuple-element.50) | data formatting | bytes 32768 | tf_op jit(solution)/shard_map/reduce_sum | solution.py:349
  76.0 1.5 %copy.87 = f32[16,256]{0,1:T(8,128)} copy(f32[16,256]{1,0:T(8,128)} %get-tuple-element.51) | data formatting | bytes 32768 | tf_op jit(solution)/shard_map/reduce_sum | solution.py:349
  77.7 1.7 %collective-permute-done.4 = bf16[16,64,128]{2,1,0:T(8,128)(2,1)S(1)} collective-permute-done((bf16[16,64,128]{2,1,0:T(8,128)(2,1)}, bf16[16,64,128]{2,1,0:T(8,128)(2,1)S(1)}, u32[]{:S(2)}, u32[]{:S(2)}) %collective-permute-start.4) | collective-permute-done | bytes 262176 | tf_op jit(solution)/shard_map/ppermute | solution.py:23
  79.4 1.5 %convolution_bitcast_fusion.2 = f32[128,256]{1,0:T(8,128)S(1)} fusion(f32[256,16,64]{0,2,1:T(8,128)S(1)} %bitcast.106, f32[256,16]{0,1:T(8,128)} %copy.83, bf16[16,64,128]{2,1,0:T(8,128)(2,1)S(1)} %collective-permute-done.2, bf16[16,64,128]{2,1,0:T(8,128)(2,1)} %collective-permute-done, bf16[16,64,128]{2,1,0:T(8,128)(2,1)S(1)} %collective-permute-done.4, ...), kind=kOutput, calls=%fused_computation.20 | convolution fusion | flops 69074944 | bytes 1982595 | tf_op jit(solution)/shard_map/jhp,hpn->nj/dot_general | solution.py:346
  81.2 2.3 %multiply_reduce_fusion.1 = (f32[256,16]{0,1:T(8,128)S(1)}, f32[256,16]{0,1:T(8,128)S(1)}, bf16[256,16,64]{0,2,1:T(8,128)(2,1)S(1)}, f32[16]{0:T(128)S(1)}) fusion(f32[256,1024]{0,1:T(8,128)S(1)} %copy.84, f32[256,16,64]{0,2,1:T(8,128)} %fusion.8, f32[256,16]{0,1:T(8,128)S(1)} %copy-done.9, bf16[256,16,64]{0,2,1:T(8,128)(2,1)S(1)} %bitcast.101, ...), kind=kOutput, calls=%fused_computation.29 | convolution fusion | flops 72474608 | bytes 5128451 | tf_op jit(solution)/shard_map/jn,hpn->jhp/dot_general | solution.py:333
  83.6 1.1 fusion.35
  84.7 1.4 %multiply_reduce_fusion.2 = f32[16]{0:T(128)S(1)} fusion(bf16[16,64,128]{2,1,0:T(8,128)(2,1)S(1)} %bitcast.104, bf16[16,64,128]{2,1,0:T(8,128)(2,1)} %copy-done.6, f32[16]{0:T(128)} %get-tuple-element.57, bf16[16,64,128]{2,1,0:T(8,128)(2,1)S(1)} %collective-permute-done.2, f32[16]{0:T(128)} %get-tuple-element.58, ...), kind=kLoop, calls=%fused_computation.49 | loop fusion | flops 1703920 | bytes 1048771 | tf_op jit(solution)/shard_map/reduce_sum | solution.py:350
  87.9 0.7 copy.97
  88.8 43.5 %matmul_scatter.1 = (bf16[1024,256]{1,0:T(8,128)(2,1)S(1)}, bf16[64,256]{1,0:T(8,128)(2,1)S(1)}, f32[8,128]{1,0:T(8,128)S(1)}) custom-call(bf16[4096,1024]{1,0:T(8,128)(2,1)} %w_hbm.3, bf16[256,1024]{1,0:T(8,128)(2,1)S(1)} %copy.96.x_ref, f32[256,256]{1,0:T(8,128)S(1)} %pad_maximum_fusion.bc_ref, f32[8,128]{1,0:T(8,128)S(1)} %select_maximum_fusion.p_ref), custom_call_target="tpu_custom_call" | custom-call | tf_op jit(solution)/shard_map/matmul_scatter/pallas_call | solution.py:264
  132.9 0.8 copy.105
  (84 shorter events, 8.5 us)
Async XLA Ops:
  0.6 50.1 %copy-start = (bf16[256,128]{1,0:T(8,128)(2,1)S(1)}, bf16[256,128]{1,0:T(8,128)(2,1)}, u32[]{:S(2)}) copy-start(bf16[256,128]{1,0:T(8,128)(2,1)} %param.17) | copy-start | bytes 196612
  1.3 1.6 %copy-start.16 = (f32[16]{0:T(128)}, f32[16]{0:T(128)S(1)}, u32[]{:S(2)}) copy-start(f32[16]{0:T(128)S(1)} %exponential_negate_fusion) | copy-start | bytes 196
  4.5 51.5 %collective-permute-start.1 = (f32[16]{0:T(128)}, f32[16]{0:T(128)}, u32[]{:S(2)}, u32[]{:S(2)}) collective-permute-start(f32[16]{0:T(128)} %fusion.39), channel_id=1, source_target_pairs={{0,4},{4,0},{8,12},{12,8},{16,20},{20,16},{24,28},{28,24},{1,5},{5... | collective-permute-start | bytes 200 | tf_op jit(solution)/shard_map/ppermute | solution.py:22
  5.0 1.0 copy-start.1
  6.0 42.1 %copy-start.13 = (f32[16]{0:T(128)}, f32[16]{0:T(128)S(1)}, u32[]{:S(2)}) copy-start(f32[16]{0:T(128)S(1)} %slice_bitcast_fusion) | copy-start | bytes 196
  6.0 42.2 %copy-start.11 = (f32[16]{0:T(128)S(1)}, f32[16]{0:T(128)}, u32[]{:S(2)}) copy-start(f32[16]{0:T(128)} %param.20) | copy-start | bytes 196
  6.0 43.0 %copy-start.5 = (bf16[256,128]{1,0:T(8,128)(2,1)S(1)}, bf16[256,128]{1,0:T(8,128)(2,1)}, u32[]{:S(2)}) copy-start(bf16[256,128]{1,0:T(8,128)(2,1)} %param.18) | copy-start | bytes 196612
  48.2 4.9 %copy-start.2 = (bf16[256,1024]{0,1:T(8,128)(2,1)}, bf16[256,1024]{0,1:T(8,128)(2,1)S(1)}, u32[]{:S(2)}) copy-start(bf16[256,1024]{0,1:T(8,128)(2,1)S(1)} %copy.76) | copy-start | bytes 1572868
  50.1 11.4 %collective-permute-start = (bf16[16,64,128]{2,1,0:T(8,128)(2,1)}, bf16[16,64,128]{2,1,0:T(8,128)(2,1)}, u32[]{:S(2)}, u32[]{:S(2)}) collective-permute-start(bf16[16,64,128]{2,1,0:T(8,128)(2,1)} %get-tuple-element.68), channel_id=1, source_target_pairs={{0,4},{4,0},{8,12},{12,8},{16,20},{20,16},{24,28},{28,24},{1,5},{5... | collective-permute-start | bytes 786440 | tf_op jit(solution)/shard_map/ppermute | solution.py:23
  53.4 10.8 %copy-start.3 = (bf16[256,1024]{0,1:T(8,128)(2,1)S(1)}, bf16[256,1024]{0,1:T(8,128)(2,1)}, u32[]{:S(2)}) copy-start(bf16[256,1024]{0,1:T(8,128)(2,1)} %copy-done.2) | copy-start | bytes 1572868
  56.0 8.3 %copy-start.10 = (f32[256,16]{0,1:T(8,128)}, f32[256,16]{0,1:T(8,128)S(1)}, u32[]{:S(2)}) copy-start(f32[256,16]{0,1:T(8,128)S(1)} %copy.75) | copy-start | bytes 49156
  56.7 7.6 %copy-start.18 = (f32[16]{0:T(128)}, f32[16]{0:T(128)S(1)}, u32[]{:S(2)}) copy-start(f32[16]{0:T(128)S(1)} %fusion.40) | copy-start | bytes 196
  56.7 3.6 %collective-permute-start.3 = (f32[16]{0:T(128)S(1)}, f32[16]{0:T(128)S(1)}, u32[]{:S(2)}, u32[]{:S(2)}) collective-permute-start(f32[16]{0:T(128)S(1)} %fusion.40), channel_id=1, source_target_pairs={{0,8},{4,12},{8,0},{12,4},{16,24},{20,28},{24,16},{28,20},{1,9},{5... | collective-permute-start | bytes 200 | tf_op jit(solution)/shard_map/ppermute | solution.py:22
  60.2 4.0 %copy-start.14 = (f32[16]{0:T(128)}, f32[16]{0:T(128)S(1)}, u32[]{:S(2)}) copy-start(f32[16]{0:T(128)S(1)} %collective-permute-done.3) | copy-start | bytes 196
  62.7 8.0 %collective-permute-start.2 = (bf16[16,64,128]{2,1,0:T(8,128)(2,1)S(1)}, bf16[16,64,128]{2,1,0:T(8,128)(2,1)S(1)}, u32[]{:S(2)}, u32[]{:S(2)}) collective-permute-start(bf16[16,64,128]{2,1,0:T(8,128)(2,1)S(1)} %fusion.41), channel_id=1, source_target_pairs={{0,8},{4,12},{8,0},{12,4},{16,24},{20,28},{24,16},{28,20},{1,9},{5... | collective-permute-start | bytes 786440 | tf_op jit(solution)/shard_map/ppermute | solution.py:23
  64.2 4.1 %copy-start.7 = (f32[256,256]{1,0:T(8,128)S(1)}, f32[256,256]{1,0:T(8,128)}, u32[]{:S(2)}) copy-start(f32[256,256]{1,0:T(8,128)} %fusion.46) | copy-start | bytes 786436
  64.2 4.1 %copy-start.8 = (pred[256,256]{1,0:T(8,128)(4,1)S(1)}, pred[256,256]{1,0:T(8,128)(4,1)}, u32[]{:S(2)}) copy-start(pred[256,256]{1,0:T(8,128)(4,1)} %iota_compare_fusion) | copy-start | bytes 196612
  68.3 2.3 %copy-start.15 = (f32[16]{0:T(128)S(1)}, f32[16]{0:T(128)}, u32[]{:S(2)}) copy-start(f32[16]{0:T(128)} %copy-done.14) | copy-start | bytes 196
  68.3 2.3 %copy-start.19 = (f32[16]{0:T(128)S(1)}, f32[16]{0:T(128)}, u32[]{:S(2)}) copy-start(f32[16]{0:T(128)} %copy-done.18) | copy-start | bytes 196
  68.3 5.8 %copy-start.4 = (bf16[1,1024,128]{2,1,0:T(8,128)(2,1)S(1)}, bf16[1,1024,128]{2,1,0:T(8,128)(2,1)}, u32[]{:S(2)}) copy-start(bf16[1,1024,128]{2,1,0:T(8,128)(2,1)} %param.23) | copy-start | bytes 786436
  70.6 10.6 %copy-start.9 = (f32[256,16]{0,1:T(8,128)S(1)}, f32[256,16]{0,1:T(8,128)}, u32[]{:S(2)}) copy-start(f32[256,16]{0,1:T(8,128)} %copy.94) | copy-start | bytes 49156
  72.6 6.8 %collective-permute-start.4 = (bf16[16,64,128]{2,1,0:T(8,128)(2,1)}, bf16[16,64,128]{2,1,0:T(8,128)(2,1)S(1)}, u32[]{:S(2)}, u32[]{:S(2)}) collective-permute-start(bf16[16,64,128]{2,1,0:T(8,128)(2,1)} %fusion.19), channel_id=1, source_target_pairs={{0,16},{4,20},{8,24},{12,28},{16,0},{20,4},{24,8},{28,12},{1,17},{... | collective-permute-start | bytes 786440 | tf_op jit(solution)/shard_map/ppermute | solution.py:23
  79.4 1.5 %copy-start.6 = (bf16[16,64,128]{2,1,0:T(8,128)(2,1)}, bf16[16,64,128]{2,1,0:T(8,128)(2,1)S(1)}, u32[]{:S(2)}) copy-start(bf16[16,64,128]{2,1,0:T(8,128)(2,1)S(1)} %collective-permute-done.4) | copy-start | bytes 786436
  81.2 6.5 %copy-start.12 = (f32[16]{0:T(128)S(1)}, f32[16]{0:T(128)}, u32[]{:S(2)}) copy-start(f32[16]{0:T(128)} %param.20) | copy-start | bytes 196
  81.2 6.5 %copy-start.17 = (f32[16]{0:T(128)S(1)}, f32[16]{0:T(128)}, u32[]{:S(2)}) copy-start(f32[16]{0:T(128)} %copy-done.16) | copy-start | bytes 196
